TPU v7x, 128 devices: a whole 4x4x4 slice. The times are simulated.
128 devices in a mesh: grp: 8 (over z, x_hi), dev: 16 (over y, x_lo, core).
Axes of the slice: x: 4 (x_hi: 2, x_lo: 2; x = x_hi * 2 + x_lo), y: 4, z: 4, core: 2. Of those that a mesh axis runs over, the one named last changes fastest.
Arguments:
- output_gradient: bfloat16 [16384, 2048], P(('grp', 'dev')), may hold values from -6 to 6
- expert_choice_index: int32 [16384, 8], P(('grp', 'dev')), may hold values from 0 to 127, all different within a row; in each aligned block of 128 rows (0 to 127, 128 to 255, ...) at most 10 rows name the same one
- routing_weight: float32 [16384, 8], P(('grp', 'dev')), may hold values from 0.05 to 0.3
- stored_gate_preact: bfloat16 [128, 1280, 1536], P(('grp', 'dev')), may hold values from -6 to 6
- gate_up_weight: bfloat16 [128, 2048, 1536], P(('grp', 'dev')), may hold values from -0.125 to 0.125
- down_weight: bfloat16 [128, 768, 2048], P(('grp', 'dev')), may hold values from -0.21875 to 0.21875
- down_first_factor: bfloat16 [128, 64, 768], P(('grp', 'dev')), may hold values from -0.21875 to 0.21875
- down_second_factor: bfloat16 [128, 64, 2048], P(('grp', 'dev')), may hold values from -0.75 to 0.75
- rotated_queries: bfloat16 [16384, 4096], P('grp', 'dev'), may hold values from -800 to 800
- rotated_keys: bfloat16 [16384, 512], P('grp'), may hold values from -4 to 4
- stored_values: bfloat16 [16384, 512], P('grp'), may hold values from -6 to 6
- output_weight: bfloat16 [4096, 2048], P('dev'), may hold values from -0.09375 to 0.09375
- output_first_factor: bfloat16 [64, 4096], P(None, 'dev'), may hold values from -0.09375 to 0.09375
- output_second_factor: bfloat16 [64, 2048], replicated, may hold values from -0.75 to 0.75
Outputs:
- first_factor_gradient: float32 [128, 64, 768], P(('grp', 'dev'))
- second_factor_gradient: float32 [128, 64, 2048], P(('grp', 'dev'))
- residual_gradient: bfloat16 [16384, 2048], P(('grp', 'dev'))
- output_first_gradient: float32 [64, 4096], P(None, 'dev')
- output_second_gradient: float32 [64, 2048], replicated
- query_gradient: float32 [16384, 4096], P('grp', 'dev')
- key_gradient: float32 [16384, 512], P(('grp', 'dev'))
- value_gradient: float32 [16384, 512], P(('grp', 'dev'))
Inputs may be any that keep to these rules, and one draw needn't show every extreme that they name: `expert_choice_index`: each row names 8 different experts; within the rows of one device no expert is named more than 10 times, a bound that some block reaches.
All inputs are finite; a program needn't handle non-finite values.
Results may differ from a plain program's by a relative error of at most 0.024.
Values may be sent and summed in bfloat16 or wider, within the bound.
A program may use at most 192 MiB of HBM per device.

v0:
```python
import jax
import jax.numpy as jnp
from jax import lax
from jax.sharding import PartitionSpec as P

QUERY_HEADS = 32
KVH = 4
HEAD_SIZE = 128


adapter_scale = 2.0
neg_big = -1e30


def contraction(left, right, left_dim, right_dim):
    return lax.dot_general(
        left, right, (((left_dim,), (right_dim,)), ((), ())), preferred_element_type=jnp.float32
    )


def expert_backward(routed_rows, saved_rows, gate_up, down_output, lowrank_first, low_b):
    width_ff = down_output.shape[0]
    pre_gate = saved_rows[:, :width_ff].astype(jnp.float32)
    pre_up = saved_rows[:, width_ff:].astype(jnp.float32)
    sigmoid = jax.nn.sigmoid(pre_gate)
    activated = pre_gate * sigmoid
    slope = sigmoid * (1.0 + pre_gate * (1.0 - sigmoid))
    hidden_activity = (activated * pre_up).astype(jnp.bfloat16)
    lowrank_input = contraction(hidden_activity, lowrank_first, 1, 1).astype(jnp.bfloat16)
    lowrank_gradient = contraction(routed_rows, low_b, 1, 1).astype(jnp.bfloat16)
    gradient_second = adapter_scale * contraction(lowrank_input, routed_rows, 0, 0)
    gradient_first = adapter_scale * contraction(lowrank_gradient, hidden_activity, 0, 0)
    hidden_gradient = contraction(routed_rows, down_output, 1, 1) + adapter_scale * jnp.dot(
        lowrank_gradient, lowrank_first, preferred_element_type=jnp.float32
    )
    grad_pre = jnp.concatenate(
        [hidden_gradient * pre_up * slope, hidden_gradient * activated], axis=1
    ).astype(jnp.bfloat16)
    return (
        contraction(grad_pre, gate_up, 1, 1).astype(jnp.bfloat16),
        gradient_first,
        gradient_second,
    )


def on_device(
    output_gradient,
    expert_choice_index,
    routing_weight,
    stored_gate_preact,
    gate_up_weight,
    down_weight,
    down_first_factor,
    down_second_factor,
    rotated_queries,
    rotated_keys,
    stored_values,
    output_weight,
    output_first_factor,
    output_second_factor,
):
    tok_rows, model_width = output_gradient.shape
    top_count = expert_choice_index.shape[1]
    grp_count = lax.axis_size("grp")
    dev_count = lax.axis_size("dev")
    experts = grp_count * dev_count
    slot_count = stored_gate_preact.shape[1]
    capacity = slot_count // experts
    assign = tok_rows * top_count
    flat_ids = expert_choice_index.reshape(assign)
    onehot = (flat_ids[:, None] == jnp.arange(experts, dtype=jnp.int32)[None, :]).astype(jnp.int32)
    before = jnp.cumsum(onehot, axis=0) - onehot
    slot_rank = jnp.sum(before * onehot, axis=1)
    cells = flat_ids * capacity + slot_rank
    scaled = (
        (routing_weight[:, :, None] * output_gradient[:, None, :].astype(jnp.float32))
        .astype(jnp.bfloat16)
        .reshape(assign, model_width)
    )
    outgoing = jnp.zeros((experts * capacity, model_width), jnp.bfloat16).at[cells].set(scaled)
    outgoing = outgoing.reshape(experts, capacity, model_width)
    incoming = lax.all_to_all(outgoing, ("grp", "dev"), split_axis=0, concat_axis=0, tiled=True)
    routed_rows = incoming.reshape(slot_count, model_width)
    grad_rows, gradient_first, gradient_second = expert_backward(
        routed_rows,
        stored_gate_preact[0],
        gate_up_weight[0],
        down_weight[0],
        down_first_factor[0],
        down_second_factor[0],
    )
    returned = lax.all_to_all(
        grad_rows.reshape(experts, capacity, model_width),
        ("grp", "dev"),
        split_axis=0,
        concat_axis=0,
        tiled=True,
    )
    picked = returned.reshape(experts * capacity, model_width)[cells]
    merged_result = jnp.sum(
        picked.reshape(tok_rows, top_count, model_width).astype(jnp.float32), axis=1
    )
    residual_gradient = (output_gradient.astype(jnp.float32) + merged_result).astype(jnp.bfloat16)
    segment_gradient = lax.all_gather(residual_gradient, "dev", axis=0, tiled=True)
    piece_len = segment_gradient.shape[0]
    device_share = rotated_queries.shape[1] // HEAD_SIZE
    group_size = QUERY_HEADS // KVH
    rank_total = output_second_factor.shape[0]
    kv_index = lax.axis_index("dev") * device_share // group_size
    key_rows = lax.dynamic_slice_in_dim(rotated_keys, kv_index * HEAD_SIZE, HEAD_SIZE, 1)
    value_rows = lax.dynamic_slice_in_dim(stored_values, kv_index * HEAD_SIZE, HEAD_SIZE, 1)
    lowrank_token = contraction(segment_gradient, output_second_factor, 1, 1).astype(jnp.bfloat16)
    head_gradient = (
        contraction(segment_gradient, output_weight, 1, 1)
        + adapter_scale
        * jnp.dot(lowrank_token, output_first_factor, preferred_element_type=jnp.float32)
    ).astype(jnp.bfloat16)
    lowrank_heads = output_first_factor.reshape(rank_total, device_share, HEAD_SIZE)
    att_scale = HEAD_SIZE ** (-0.5)
    block_rows = min(512, piece_len)
    grad_key_sum = jnp.zeros((piece_len, HEAD_SIZE), jnp.float32)
    grad_value_sum = jnp.zeros((piece_len, HEAD_SIZE), jnp.float32)
    row_contrib = jnp.zeros((rank_total, device_share * HEAD_SIZE), jnp.float32)
    column_contrib = jnp.zeros((rank_total, model_width), jnp.float32)
    query_parts = []
    for number in range(piece_len // block_rows):
        first_row = number * block_rows
        last_row = first_row + block_rows
        query_block = rotated_queries[first_row:last_row].reshape(
            block_rows, device_share, HEAD_SIZE
        )
        grad_block = head_gradient[first_row:last_row].reshape(block_rows, device_share, HEAD_SIZE)
        key_part = key_rows[:last_row]
        value_part = value_rows[:last_row]
        scores = (
            jnp.einsum("qhd,kd->hqk", query_block, key_part, preferred_element_type=jnp.float32)
            * att_scale
        )
        positions = first_row + jnp.arange(block_rows, dtype=jnp.int32)
        causal = positions[:, None] >= jnp.arange(last_row, dtype=jnp.int32)[None, :]
        scores = jnp.where(causal[None, :, :], scores, neg_big)
        probs_full = jnp.exp(scores - jnp.max(scores, axis=2, keepdims=True))
        probs_full = probs_full / jnp.sum(probs_full, axis=2, keepdims=True)
        probs_low = probs_full.astype(jnp.bfloat16)
        attended = jnp.einsum(
            "hqk,kd->qhd", probs_low, value_part, preferred_element_type=jnp.float32
        ).astype(jnp.bfloat16)
        grad_probs = jnp.einsum(
            "qhd,kd->hqk", grad_block, value_part, preferred_element_type=jnp.float32
        )
        row_delta = jnp.sum(grad_block.astype(jnp.float32) * attended.astype(jnp.float32), axis=2)
        grad_scores = (probs_full * (grad_probs - row_delta.T[:, :, None])).astype(jnp.bfloat16)
        query_parts.append(
            att_scale
            * jnp.einsum("hqk,kd->qhd", grad_scores, key_part, preferred_element_type=jnp.float32)
        )
        grad_key_sum = grad_key_sum.at[:last_row].add(
            att_scale
            * jnp.einsum(
                "hqk,qhd->kd", grad_scores, query_block, preferred_element_type=jnp.float32
            )
        )
        grad_value_sum = grad_value_sum.at[:last_row].add(
            jnp.einsum("hqk,qhd->kd", probs_low, grad_block, preferred_element_type=jnp.float32)
        )
        row_contrib = row_contrib + contraction(
            lowrank_token[first_row:last_row],
            attended.reshape(block_rows, device_share * HEAD_SIZE),
            0,
            0,
        )
        flattened = jnp.einsum(
            "qhd,rhd->qhr", attended, lowrank_heads, preferred_element_type=jnp.float32
        ).astype(jnp.bfloat16)
        column_contrib = column_contrib + jnp.einsum(
            "qhr,qc->rc",
            flattened,
            segment_gradient[first_row:last_row],
            preferred_element_type=jnp.float32,
        )
    query_gradient = jnp.concatenate(query_parts, axis=0).reshape(
        piece_len, device_share * HEAD_SIZE
    )
    output_first_gradient = lax.psum(
        (adapter_scale * row_contrib).astype(jnp.bfloat16), "grp"
    ).astype(jnp.float32)
    output_second_gradient = lax.psum(adapter_scale * column_contrib, ("grp", "dev"))
    empty = jnp.zeros((piece_len, KVH * HEAD_SIZE), jnp.float32)
    key_term = lax.dynamic_update_slice(empty, grad_key_sum, (0, kv_index * HEAD_SIZE))
    value_term = lax.dynamic_update_slice(empty, grad_value_sum, (0, kv_index * HEAD_SIZE))
    key_gradient, value_gradient = (
        lax.psum_scatter(
            key_term.astype(jnp.bfloat16), "dev", scatter_dimension=0, tiled=True
        ).astype(jnp.float32),
        lax.psum_scatter(
            value_term.astype(jnp.bfloat16), "dev", scatter_dimension=0, tiled=True
        ).astype(jnp.float32),
    )
    return (
        gradient_first[None],
        gradient_second[None],
        residual_gradient,
        output_first_gradient,
        output_second_gradient,
        query_gradient,
        key_gradient,
        value_gradient,
    )


def solution(mesh):
    in_specs = (
        P(("grp", "dev"), None),
        P(("grp", "dev"), None),
        P(("grp", "dev"), None),
        P(("grp", "dev"), None, None),
        P(("grp", "dev"), None, None),
        P(("grp", "dev"), None, None),
        P(("grp", "dev"), None, None),
        P(("grp", "dev"), None, None),
        P("grp", "dev"),
        P("grp", None),
        P("grp", None),
        P("dev", None),
        P(None, "dev"),
        P(),
    )
    out_specs = (
        P(("grp", "dev"), None, None),
        P(("grp", "dev"), None, None),
        P(("grp", "dev"), None),
        P(None, "dev"),
        P(),
        P("grp", "dev"),
        P(("grp", "dev"), None),
        P(("grp", "dev"), None),
    )
    return jax.shard_map(
        on_device, mesh=mesh, in_specs=in_specs, out_specs=out_specs, check_vma=False
    )
```

profile of v0, /device:TPU:1, one launch (start us, length us, event | category | flops | bytes accessed | tf_op | source)
XLA Modules:
  0.0 718.6 jit_solution(16234337022996242933)
XLA Ops:
  12.4 2.1 convert_element_type.174
  16.2 10.5 %scatter_custom_fusion = bf16[1280,2048]{1,0:T(8,128)(2,1)} fusion(s32[1024]{0:T(1024)S(1)} %bitcast.379, f32[128,2048]{1,0:T(8,128)} %convert_element_type.174, f32[1024]{0:T(1024)S(1)} %mul.209, bf16[]{:T(256)} %constant.250.clone.1), kind=kCustom, calls=%fused_computation.28 | custom fusion | flops 4194304 | bytes 6295554 | tf_op jit(solution)/shard_map/scatter | solution.py:80
  26.6 9.5 %reshape.411 = bf16[128,10,2048]{2,1,0:T(8,128)(2,1)} reshape(bf16[1280,2048]{1,0:T(8,128)(2,1)} %scatter_custom_fusion) | data formatting | bytes 10485760 | tf_op jit(solution)/shard_map/reshape | solution.py:81
  36.2 12.4 %all-to-all-start = ((bf16[128,10,2048]{2,1,0:T(8,128)(2,1)}), bf16[128,10,2048]{2,1,0:T(8,128)(2,1)}, u32[]{:S(2)}, u32[]{:S(2)}) async-start(bf16[128,10,2048]{2,1,0:T(8,128)(2,1)} %reshape.411), calls=%async_computation | async-start | bytes 16777216 | tf_op jit(solution)/shard_map/all_to_all | solution.py:82
  48.6 6.2 copy.100
  54.9 94.9 %all-to-all-done = bf16[128,10,2048]{2,1,0:T(8,128)(2,1)} async-done(((bf16[128,10,2048]{2,1,0:T(8,128)(2,1)}), bf16[128,10,2048]{2,1,0:T(8,128)(2,1)}, u32[]{:S(2)}, u32[]{:S(2)}) %all-to-all-start) | async-done | bytes 5242912 | tf_op jit(solution)/shard_map/all_to_all | solution.py:82
  149.8 9.8 %reshape.412 = bf16[1280,2048]{1,0:T(8,128)(2,1)} reshape(bf16[128,10,2048]{2,1,0:T(8,128)(2,1)} %all-to-all-done) | data formatting | bytes 10485760 | tf_op jit(solution)/shard_map/reshape | solution.py:83
  159.6 4.3 convolution_convert_fusion.3
  164.0 4.3 fusion.35
  168.3 3.8 fusion.24
  172.2 10.2 %convolution_convert_fusion = bf16[1280,2048]{1,0:T(8,128)(2,1)} fusion(bf16[1,2048,1536]{2,1,0:T(8,128)(2,1)S(1)} %bitcast.382, bf16[1280,768]{0,1:T(8,128)(2,1)S(1)} %get-tuple-element.149, bf16[1280,768]{0,1:T(8,128)(2,1)S(1)} %get-tuple-element.148), kind=kOutput, calls=%fused_computation.14 | convolution fusion | flops 8063549440 | bytes 15466496 | tf_op jit(solution)/shard_map/dot_general | solution.py:16
  182.4 9.5 %reshape.413 = bf16[128,10,2048]{2,1,0:T(8,128)(2,1)} reshape(bf16[1280,2048]{1,0:T(8,128)(2,1)} %convolution_convert_fusion) | data formatting | bytes 10485760 | tf_op jit(solution)/shard_map/reshape | solution.py:93
  191.9 15.0 %all-to-all-start.1 = ((bf16[128,10,2048]{2,1,0:T(8,128)(2,1)}), bf16[128,10,2048]{2,1,0:T(8,128)(2,1)}, u32[]{:S(2)}, u32[]{:S(2)}) async-start(bf16[128,10,2048]{2,1,0:T(8,128)(2,1)} %reshape.413), calls=%async_computation.1 | async-start | bytes 16777216 | tf_op jit(solution)/shard_map/all_to_all | solution.py:92
  206.9 101.3 %all-to-all-done.1 = bf16[128,10,2048]{2,1,0:T(8,128)(2,1)} async-done(((bf16[128,10,2048]{2,1,0:T(8,128)(2,1)}), bf16[128,10,2048]{2,1,0:T(8,128)(2,1)}, u32[]{:S(2)}, u32[]{:S(2)}) %all-to-all-start.1) | async-done | bytes 5242912 | tf_op jit(solution)/shard_map/all_to_all | solution.py:92
  308.2 9.8 %reshape.414 = bf16[1280,2048]{1,0:T(8,128)(2,1)} reshape(bf16[128,10,2048]{2,1,0:T(8,128)(2,1)} %all-to-all-done.1) | data formatting | bytes 10485760 | tf_op jit(solution)/shard_map/reshape | solution.py:99
  318.1 12.0 %gather_fusion = bf16[1024,2048]{1,0:T(8,128)(2,1)} fusion(bf16[1280,2048]{1,0:T(8,128)(2,1)} %reshape.414, s32[1024]{0:T(1024)S(1)} %broadcast_clamp_fusion), kind=kCustom, calls=%fused_computation | custom fusion | bytes 8392704 | tf_op jit(solution)/shard_map/gather | solution.py:99
  330.0 5.1 convert_reduce_fusion
  336.1 8.8 %reduce-scatter.3.cloned.1.call-start = ((), (), s32[]{:S(2)}) async-start(), calls=%async_computation.6 | async-start | bytes 2228224 | tf_op jit(solution)/shard_map/reduce_scatter | solution.py:192
  351.5 4.6 fusion.177
  356.0 2.9 fusion.67
  360.3 3.2 fusion.176
  364.1 6.1 fusion.178
  370.2 3.8 fusion.43
  377.1 1.8 iota_compare_fusion
  378.9 8.2 %fusion.179 = (f32[2,512]{1,0:T(2,128)S(1)}, f32[2,512,2048]{1,2,0:T(8,128)}) fusion(pred[512,2048]{0,1:T(8,128)(4,1)} %iota_compare_fusion, bf16[512,2,128]{0,2,1:T(8,128)(2,1)S(1)} %bitcast.363, bf16[2048,512]{1,0:T(8,128)(2,1)} %param.43, s32[]{:T(128)S(6)} %select_n.40), kind=kOutput, calls=%fused_computation.246 | convolution fusion | flops 545261568 | bytes 10227716 | tf_op jit(solution)/shard_map/sub | solution.py:142
  387.1 4.7 fusion.33
  391.8 2.0 copy-done.2
  394.6 6.1 fusion.184
  400.8 2.6 convolution_convert_fusion.2
  412.2 3.0 copy-done.20
  420.1 2.1 fusion.46
  422.3 1.9 fusion.83
  433.8 3.0 fusion.86
  436.7 5.4 fusion.54
  446.9 38.8 %psum.14 = bf16[64,256]{1,0:T(8,128)(2,1)S(1)} all-reduce(bf16[64,256]{1,0:T(8,128)(2,1)S(1)} %fusion.88), channel_id=1, replica_groups=mesh['grp'=8,'dev'=16] {'grp'}, use_global_device_ids=true, to_apply=%region_13.14 | all-reduce | flops 16384 | bytes 65536 | tf_op jit(solution)/shard_map/psum | solution.py:184
  487.5 2.0 fusion.69
  489.6 2.3 fusion.74
  491.8 2.1 fusion.59
  493.9 2.1 convolution_add_fusion.2
  496.0 2.2 convolution_add_fusion.1
  498.2 2.9 fusion.55
  501.1 2.6 fusion.68
  503.7 2.6 fusion.73
  506.4 3.2 pad_maximum_fusion
  509.6 2.9 copy.142
  514.1 42.5 %reduce-scatter.5.cloned.1.call-done = bf16[128,512]{1,0:T(8,128)(2,1)} async-done(((bf16[2048,512]{1,0:T(8,128)(2,1)}), bf16[128,512]{1,0:T(8,128)(2,1)}) %reduce-scatter.5.cloned.1.call-update) | async-done | bytes 131088 | tf_op jit(solution)/shard_map/reduce_scatter | solution.py:195
  558.2 151.8 %all-reduce.4.cloned.1.call-done = f32[64,2048]{1,0:T(8,128)} async-done(((f32[64,2048]{1,0:T(8,128)}), f32[64,2048]{1,0:T(8,128)}) %all-reduce.4.cloned.1.call-update) | async-done | bytes 524304 | tf_op jit(solution)/shard_map/psum | solution.py:187
  710.0 1.9 copy.217
  (213 shorter events, 52.9 us)
Async XLA Ops:
  7.2 156.8 %copy-start = (bf16[1,768,2048]{2,1,0:T(8,128)(2,1)S(1)}, bf16[1,768,2048]{2,1,0:T(8,128)(2,1)}, u32[]{:S(2)}) copy-start(bf16[1,768,2048]{2,1,0:T(8,128)(2,1)} %param.39) | copy-start | bytes 9437188
  7.2 7.4 %copy-start.60 = (f32[128,8]{0,1:T(8,128)S(1)}, f32[128,8]{0,1:T(8,128)}, u32[]{:S(2)}) copy-start(f32[128,8]{0,1:T(8,128)} %param.36) | copy-start | bytes 12292
  36.2 113.6 %all-to-all-start = ((bf16[128,10,2048]{2,1,0:T(8,128)(2,1)}), bf16[128,10,2048]{2,1,0:T(8,128)(2,1)}, u32[]{:S(2)}, u32[]{:S(2)}) async-start(bf16[128,10,2048]{2,1,0:T(8,128)(2,1)} %reshape.411), calls=%async_computation | async-start | bytes 16777216 | tf_op jit(solution)/shard_map/all_to_all | solution.py:82
  54.9 104.8 %copy-start.53 = (bf16[1,64,2048]{2,1,0:T(8,128)(2,1)S(1)}, bf16[1,64,2048]{2,1,0:T(8,128)(2,1)}, u32[]{:S(2)}) copy-start(bf16[1,64,2048]{2,1,0:T(8,128)(2,1)} %param.41) | copy-start | bytes 786436
  159.6 4.4 copy-start.4
  164.0 4.3 copy-start.51
  164.0 4.3 copy-start.22
  164.0 4.3 copy-start.59
  164.0 8.1 %slice-start.4 = ((s8[6291456]{0:T(1024)(128)(4,1)}), s8[4194304]{0:T(1024)(128)(4,1)S(1)}, s32[]{:S(2)}) async-start(s8[6291456]{0:T(1024)(128)(4,1)} %bitcast.381), calls=%async_computation.12 | async-start | bytes 8388608
  168.3 3.8 slice-start.5
  191.9 116.3 %all-to-all-start.1 = ((bf16[128,10,2048]{2,1,0:T(8,128)(2,1)}), bf16[128,10,2048]{2,1,0:T(8,128)(2,1)}, u32[]{:S(2)}, u32[]{:S(2)}) async-start(bf16[128,10,2048]{2,1,0:T(8,128)(2,1)} %reshape.413), calls=%async_computation.1 | async-start | bytes 16777216 | tf_op jit(solution)/shard_map/all_to_all | solution.py:92
  206.9 187.7 %all-gather.2.cloned.1.call-start = ((), (), s32[]{:S(2)}) async-start(), calls=%async_computation.4 | async-start | bytes 8912896 | tf_op jit(solution)/shard_map/all_gather | solution.py:104
  330.0 5.1 copy-start.29
  335.1 11.0 %copy-start.38 = (bf16[2048,256]{1,0:T(8,128)(2,1)S(1)}, bf16[2048,256]{1,0:T(8,128)(2,1)}, u32[]{:S(2)}) copy-start(bf16[2048,256]{1,0:T(8,128)(2,1)} %param.42) | copy-start | bytes 3145732
  336.1 176.4 %reduce-scatter.3.cloned.1.call-start = ((), (), s32[]{:S(2)}) async-start(), calls=%async_computation.6 | async-start | bytes 2228224 | tf_op jit(solution)/shard_map/reduce_scatter | solution.py:192
  346.0 5.4 copy-start.15
  348.0 8.0 %copy-start.45 = (bf16[512,256]{0,1:T(8,128)(2,1)}, bf16[512,256]{0,1:T(8,128)(2,1)S(1)}, u32[]{:S(2)}) copy-start(bf16[512,256]{0,1:T(8,128)(2,1)S(1)} %copy.185) | copy-start | bytes 786436
  348.1 10.8 %copy-start.36 = (bf16[1024,128]{0,1:T(8,128)(2,1)}, bf16[1024,128]{0,1:T(8,128)(2,1)S(1)}, u32[]{:S(2)}) copy-start(bf16[1024,128]{0,1:T(8,128)(2,1)S(1)} %copy.189) | copy-start | bytes 786436
  348.3 15.8 %copy-start.32 = (bf16[512,256]{0,1:T(8,128)(2,1)}, bf16[512,256]{0,1:T(8,128)(2,1)S(1)}, u32[]{:S(2)}) copy-start(bf16[512,256]{0,1:T(8,128)(2,1)S(1)} %copy.186) | copy-start | bytes 786436
  348.5 25.5 %copy-start.30 = (bf16[1536,128]{0,1:T(8,128)(2,1)}, bf16[1536,128]{0,1:T(8,128)(2,1)S(1)}, u32[]{:S(2)}) copy-start(bf16[1536,128]{0,1:T(8,128)(2,1)S(1)} %copy.190) | copy-start | bytes 1179652
  349.5 10.8 %copy-start.39 = (bf16[512,256]{0,1:T(8,128)(2,1)}, bf16[512,256]{0,1:T(8,128)(2,1)S(1)}, u32[]{:S(2)}) copy-start(bf16[512,256]{0,1:T(8,128)(2,1)S(1)} %copy.184) | copy-start | bytes 786436
  356.0 4.3 copy-start.55
  358.9 11.3 %copy-start.10 = (bf16[2,512,1024]{1,2,0:T(8,128)(2,1)}, bf16[2,512,1024]{1,2,0:T(8,128)(2,1)S(1)}, u32[]{:S(2)}) copy-start(bf16[2,512,1024]{1,2,0:T(8,128)(2,1)S(1)} %fusion.67) | copy-start | bytes 6291460
  375.3 3.6 copy-start.34
  387.1 6.7 copy-start.16
  394.6 6.2 copy-start.5
  394.6 6.2 copy-start.54
  404.0 4.3 slice-start
  405.0 3.4 copy-start.41
  405.0 5.6 copy-start.43
  405.0 7.3 %copy-start.48 = (bf16[512,256]{0,1:T(8,128)(2,1)}, bf16[512,256]{0,1:T(8,128)(2,1)S(1)}, u32[]{:S(2)}) copy-start(bf16[512,256]{0,1:T(8,128)(2,1)S(1)} %get-tuple-element.154) | copy-start | bytes 786436
  406.1 3.1 copy-start.17
  407.3 3.2 slice-start.2
  410.5 9.6 %copy-start.6 = (bf16[2,512,2048]{1,2,0:T(8,128)(2,1)}, bf16[2,512,2048]{1,2,0:T(8,128)(2,1)S(1)}, u32[]{:S(2)}) copy-start(bf16[2,512,2048]{1,2,0:T(8,128)(2,1)S(1)} %fusion.5) | copy-start | bytes 12582916
  411.2 4.0 copy-start.20
  411.2 4.0 copy-start.37
  412.2 5.1 copy-start.8
  422.2 134.4 %reduce-scatter.5.cloned.1.call-start = ((), (), s32[]{:S(2)}) async-start(), calls=%async_computation.7 | async-start | bytes 2228224 | tf_op jit(solution)/shard_map/reduce_scatter | solution.py:195
  422.3 5.7 copy-start.11
  422.3 5.7 copy-start.49
  422.3 6.4 copy-start.44
  433.7 276.3 %all-reduce.4.cloned.1.call-start = ((), (), s32[]{:S(2)}) async-start(), calls=%async_computation.5 | async-start | bytes 1048576 | tf_op jit(solution)/shard_map/psum | solution.py:187
  436.7 50.8 %copy-start.19 = (bf16[2,512,512]{1,2,0:T(8,128)(2,1)S(1)}, bf16[2,512,512]{1,2,0:T(8,128)(2,1)}, u32[]{:S(2)}) copy-start(bf16[2,512,512]{1,2,0:T(8,128)(2,1)} %copy-done.18) | copy-start | bytes 3145732
  442.1 47.4 %copy-start.13 = (bf16[2,512,1024]{1,2,0:T(8,128)(2,1)S(1)}, bf16[2,512,1024]{1,2,0:T(8,128)(2,1)}, u32[]{:S(2)}) copy-start(bf16[2,512,1024]{1,2,0:T(8,128)(2,1)} %copy-done.12) | copy-start | bytes 6291460
  446.9 47.0 %copy-start.57 = (bf16[512,64]{0,1:T(8,128)(2,1)S(1)}, bf16[512,64]{0,1:T(8,128)(2,1)}, u32[]{:S(2)}) copy-start(bf16[512,64]{0,1:T(8,128)(2,1)} %fusion.83) | copy-start | bytes 196612
  489.6 6.4 copy-start.56
  496.0 5.1 copy-start.9
  506.4 205.6 %copy-start.1 = (bf16[1,768,2048]{2,1,0:T(8,128)(2,1)S(1)}, bf16[1,768,2048]{2,1,0:T(8,128)(2,1)}, u32[]{:S(2)}) copy-start(bf16[1,768,2048]{2,1,0:T(8,128)(2,1)} %param.39) | copy-start | bytes 9437188
  (25 other events, 47.1 us)
Sparse Core Ops, SparseCore 0:
  336.2 57.9 all-gather.1
  422.3 67.4 reduce-scatter.2
  492.3 64.2 reduce-scatter.4
  561.8 148.2 all-reduce.3
where the time goes:
time: 727 us; the launch traced here: 719 us
  waiting for transfers between devices  391 us (54%)
  matrix products  108 us (15%)
  local copies, waits for them, and re-layouts  84 us (12%)
  other arithmetic  45.6 us (6%)
  blocking collectives  38.8 us (5%)
  starting transfers between devices  36.4 us (5%)
  between operations  14.9 us (2%)
    psum x1, waiting for transfers between devices, on_device(): lax.psum(adapter_scale * column_contrib, ('grp', 'dev'))  152 us
    all_to_all x1, waiting for transfers between devices, on_device(): lax.all_to_all(grad_rows.reshape(experts, capacity, model_width), ('grp',...  101 us
    all_to_all x1, waiting for transfers between devices, on_device(): lax.all_to_all(outgoing, ('grp', 'dev'), split_axis=0, concat_axis=0, til...  94.9 us
    reduce_scatter x1, waiting for transfers between devices, on_device(): lax.psum_scatter(value_term.astype(jnp.bfloat16), 'dev', scatter_dimensio...  42.5 us
    dot_general x11, matrix products, contraction(): lax.dot_general(left, right, (((left_dim,), (right_dim,)), ((), ())), pre...  40.8 us
    psum x1, blocking collectives, on_device(): lax.psum((adapter_scale * row_contrib).astype(jnp.bfloat16), 'grp')  38.8 us
    unnamed x146, local copies, waits for them, and re-layouts  28.2 us
    sub x4, matrix products, on_device(): probs_full = jnp.exp(scores - jnp.max(scores, axis=2, keepdims=True))  22 us
  transfers between devices with their start and end apart: 6, of which 4 were waited for; matrix products, arithmetic and copies ran while one was open for 15% of the time, Pallas kernels for 0%

commit v1 on v0

v1 whole, which is shorter than its diff:
```python
import functools

import jax
import jax.numpy as jnp
from jax import lax
from jax.experimental import pallas as pl
from jax.experimental.pallas import tpu as pltpu
from jax.sharding import PartitionSpec as P

QUERY_HEADS = 32
KVH = 4
HEAD_SIZE = 128
MESH = pl.DeviceIdType.MESH
ALL = ("grp", "dev")

adapter_scale = 2.0
neg_big = -1e30
f32 = jnp.float32
bf16 = jnp.bfloat16


def contraction(left, right, left_dim, right_dim):
    return lax.dot_general(
        left, right, (((left_dim,), (right_dim,)), ((), ())), preferred_element_type=f32
    )


def dispatch_kernel(capacity, x_ref, idx_ref, w_ref, out_ref, cells_ref, rows, tok_v, wt_v, tok_s, wt_s, sems):
    tokens, width = x_ref.shape
    sub = width // 128
    per_step = out_ref.shape[0] // capacity
    step = pl.program_id(0)

    @pl.when(step == 0)
    def _():
        for b in range(sub):
            rows[pl.ds(b, tokens, stride=sub), :] = x_ref[:, b * 128 : (b + 1) * 128].astype(f32)
        shape = (tokens, 128)
        t_iota = lax.broadcasted_iota(jnp.int32, shape, 0)
        e_iota = lax.broadcasted_iota(jnp.int32, shape, 1)
        idx = idx_ref[...]
        w = w_ref[...]
        named = jnp.zeros(shape, f32)
        weight = jnp.zeros(shape, f32)
        for k in range(idx.shape[1]):
            hit = idx[:, k : k + 1] == e_iota
            named = named + jnp.where(hit, 1.0, 0.0)
            weight = weight + jnp.where(hit, w[:, k : k + 1], 0.0)
        earlier = jnp.where(t_iota > e_iota, 1.0, 0.0).astype(bf16)
        rank = jnp.dot(earlier, named.astype(bf16), preferred_element_type=f32)
        t_float = t_iota.astype(f32)
        for c in range(capacity):
            mine = jnp.logical_and(named > 0.5, rank == float(c))
            tok_v[c : c + 1, :] = jnp.sum(
                jnp.where(mine, t_float, 0.0), axis=0, keepdims=True
            ).astype(jnp.int32)
            wt_v[c : c + 1, :] = jnp.sum(jnp.where(mine, weight, 0.0), axis=0, keepdims=True)
        cells = jnp.zeros(shape, f32)
        for k in range(idx.shape[1]):
            hit = idx[:, k : k + 1] == e_iota
            place = jnp.sum(jnp.where(hit, rank, 0.0), axis=1, keepdims=True)
            place = place + float(capacity) * idx[:, k : k + 1].astype(f32)
            cells = cells + jnp.where(e_iota == k, place, 0.0)
        cells_ref[...] = cells.astype(jnp.int32)
        one = pltpu.make_async_copy(tok_v, tok_s, sems.at[0])
        two = pltpu.make_async_copy(wt_v, wt_s, sems.at[1])
        one.start()
        two.start()
        one.wait()
        two.wait()

    def expert(j, carry):
        e = step * per_step + j
        for c in range(capacity):
            start = pl.multiple_of(tok_s[c, e] * sub, sub)
            out_ref[j * capacity + c] = (rows[pl.ds(start, sub), :] * wt_s[c, e]).astype(bf16)
        return carry

    lax.fori_loop(0, per_step, expert, 0, unroll=2)


def dispatch(x, idx, w, experts, capacity):
    tokens, width = x.shape
    sub = width // 128
    steps = 8
    slots = experts * capacity
    pad = -(-capacity // 8) * 8
    return pl.pallas_call(
        functools.partial(dispatch_kernel, capacity),
        grid=(steps,),
        out_shape=(
            jax.ShapeDtypeStruct((slots, sub, 128), bf16),
            jax.ShapeDtypeStruct((tokens, 128), jnp.int32),
        ),
        in_specs=[
            pl.BlockSpec((tokens, width), lambda i: (0, 0)),
            pl.BlockSpec(idx.shape, lambda i: (0, 0)),
            pl.BlockSpec(w.shape, lambda i: (0, 0)),
        ],
        out_specs=(
            pl.BlockSpec((slots // steps, sub, 128), lambda i: (i, 0, 0)),
            pl.BlockSpec((tokens, 128), lambda i: (0, 0)),
        ),
        scratch_shapes=[
            pltpu.VMEM((tokens * sub, 128), f32),
            pltpu.VMEM((pad, 128), jnp.int32),
            pltpu.VMEM((pad, 128), f32),
            pltpu.SMEM((pad, 128), jnp.int32),
            pltpu.SMEM((pad, 128), f32),
            pltpu.SemaphoreType.DMA((2,)),
        ],
        compiler_params=pltpu.CompilerParams(dimension_semantics=("arbitrary",)),
        name="dispatch",
    )(x, idx, w)


def expert_kernel(r_ref, s_ref, g_ref, d_ref, a_ref, b_ref, out_ref, first_ref, second_ref, wide, rows):
    count, sub, _ = r_ref.shape
    ff = d_ref.shape[0]

    @pl.when(pl.program_id(0) == 0)
    def _():
        first_ref[...] = jnp.zeros_like(first_ref)
        second_ref[...] = jnp.zeros_like(second_ref)

    wide[...] = r_ref[...].astype(f32).reshape(count * sub, 128)
    for b in range(sub):
        rows[:, b * 128 : (b + 1) * 128] = wide[pl.ds(b, count, stride=sub), :].astype(bf16)
    x = rows[...]
    pre_gate = s_ref[:, :ff].astype(f32)
    pre_up = s_ref[:, ff:].astype(f32)
    sigmoid = jax.nn.sigmoid(pre_gate)
    activated = pre_gate * sigmoid
    slope = sigmoid * (1.0 + pre_gate * (1.0 - sigmoid))
    hidden = (activated * pre_up).astype(bf16)
    low_in = contraction(hidden, a_ref[...], 1, 1).astype(bf16)
    low_grad = contraction(x, b_ref[...], 1, 1).astype(bf16)
    second_ref[...] += adapter_scale * contraction(low_in, x, 0, 0)
    first_ref[...] += adapter_scale * contraction(low_grad, hidden, 0, 0)
    grad_hidden = contraction(x, d_ref[...], 1, 1) + adapter_scale * jnp.dot(
        low_grad, a_ref[...], preferred_element_type=f32
    )
    left = (grad_hidden * (pre_up * slope)).astype(bf16)
    right = (grad_hidden * activated).astype(bf16)
    for b in range(0, sub, 2):
        at = slice(b * 128, (b + 2) * 128)
        res = contraction(left, g_ref[at, :ff], 1, 1) + contraction(right, g_ref[at, ff:], 1, 1)
        wide[pl.ds(b, count, stride=sub), :] = res[:, :128]
        wide[pl.ds(b + 1, count, stride=sub), :] = res[:, 128:]
    out_ref[...] = wide[...].reshape(count, sub, 128).astype(bf16)


def experts_backward(routed, saved, gate_up, down, first, second, count):
    slots, sub, _ = routed.shape
    ff, width = down.shape
    rank = first.shape[0]
    once = pl.Buffered(1)
    whole = lambda shape: pl.BlockSpec(shape, lambda i: (0, 0), pipeline_mode=once)
    return pl.pallas_call(
        expert_kernel,
        grid=(slots // count,),
        out_shape=(
            jax.ShapeDtypeStruct((slots, sub, 128), bf16),
            jax.ShapeDtypeStruct((rank, ff), f32),
            jax.ShapeDtypeStruct((rank, width), f32),
        ),
        in_specs=[
            pl.BlockSpec((count, sub, 128), lambda i: (i, 0, 0)),
            pl.BlockSpec((count, 2 * ff), lambda i: (i, 0)),
            whole(gate_up.shape),
            whole(down.shape),
            whole(first.shape),
            whole(second.shape),
        ],
        out_specs=(
            pl.BlockSpec((count, sub, 128), lambda i: (i, 0, 0)),
            pl.BlockSpec((rank, ff), lambda i: (0, 0)),
            pl.BlockSpec((rank, width), lambda i: (0, 0)),
        ),
        scratch_shapes=[pltpu.VMEM((count * sub, 128), f32), pltpu.VMEM((count, width), bf16)],
        compiler_params=pltpu.CompilerParams(
            dimension_semantics=("arbitrary",), vmem_limit_bytes=56 << 20
        ),
        cost_estimate=pl.CostEstimate(flops=13_500_000_000, bytes_accessed=24_000_000, transcendentals=0),
        name="experts",
    )(routed, saved, gate_up, down, first, second)


def combine_kernel(cells_ref, x_ref, r_ref, out_ref, rows):
    tokens, width = x_ref.shape
    sub = width // 128
    top = cells_ref.shape[1]

    def token(t, carry):
        total = r_ref[cells_ref[t, 0]].astype(f32)
        for k in range(1, top):
            total = total + r_ref[cells_ref[t, k]].astype(f32)
        rows[pl.ds(pl.multiple_of(t * sub, sub), sub), :] = total
        return carry

    lax.fori_loop(0, tokens, token, 0, unroll=4)
    for b in range(sub):
        at = slice(b * 128, (b + 1) * 128)
        out_ref[:, at] = (
            x_ref[:, at].astype(f32) + rows[pl.ds(b, tokens, stride=sub), :]
        ).astype(bf16)


def combine(cells, x, returned):
    tokens, width = x.shape
    return pl.pallas_call(
        combine_kernel,
        out_shape=jax.ShapeDtypeStruct(x.shape, bf16),
        in_specs=[
            pl.BlockSpec(memory_space=pltpu.SMEM),
            pl.BlockSpec(memory_space=pltpu.VMEM),
            pl.BlockSpec(memory_space=pltpu.VMEM),
        ],
        out_specs=pl.BlockSpec(memory_space=pltpu.VMEM),
        scratch_shapes=[pltpu.VMEM((tokens * width // 128, 128), f32)],
        name="combine",
    )(cells, x, returned)


def gather_kernel(x_ref, y_ref, spare, us, ds, xs, cs, ur, dr, xr, cr, lsem):
    g = lax.axis_index("grp")
    d = lax.axis_index("dev")
    y = d // 4
    xl = (d // 2) % 2
    c = d % 2
    half = x_ref.shape[0] // 2

    def idx(yy, xx):
        return yy * 4 + xx * 2 + c

    px = 1 - xl
    up, dn, op = (y + 1) % 4, (y + 3) % 4, (y + 2) % 4
    to_up, to_dn, to_x = (g, idx(up, xl)), (g, idx(dn, xl)), (g, idx(y, px))
    to_c = (g, y * 4 + xl * 2 + (1 - c))
    barrier = pltpu.get_barrier_semaphore()
    for target in (to_up, to_dn, to_x, to_c):
        pl.semaphore_signal(barrier, inc=1, device_id=target, device_id_type=MESH)
    pl.semaphore_wait(barrier, 4)
    A, B = 0, 1

    def part(h):
        return x_ref.at[pl.ds(h * half, half)]

    def at(o, h):
        return y_ref.at[o, pl.ds(h * half, half)]

    mine = idx(y, xl)
    sends = []
    order = []

    def send(src, o, h, target, ssem, rsem):
        copy = pltpu.make_async_remote_copy(
            src_ref=src, dst_ref=at(o, h), send_sem=ssem, recv_sem=rsem,
            device_id=target, device_id_type=MESH,
        )
        copy.start()
        sends.append(copy)

    def arrived(o, h, sem):
        pltpu.make_async_remote_copy(
            src_ref=at(o, h), dst_ref=at(o, h), send_sem=spare, recv_sem=sem,
            device_id=to_c, device_id_type=MESH,
        ).wait_recv()

    def across(src, o, h):
        i = len(order)
        order.append((o, h))
        send(src, o, h, to_c, cs.at[i], cr.at[i])

    own = pltpu.make_async_copy(x_ref, y_ref.at[mine], lsem)
    own.start()
    send(part(A), mine, A, to_dn, ds.at[0], ur.at[0])
    send(part(B), mine, B, to_up, us.at[0], dr.at[0])
    send(part(A), mine, A, to_x, xs.at[0], xr.at[0])
    send(part(B), mine, B, to_dn, ds.at[1], ur.at[1])
    send(part(A), mine, A, to_up, us.at[1], dr.at[1])
    send(part(B), mine, B, to_x, xs.at[1], xr.at[1])
    across(part(A), mine, A)
    across(part(B), mine, B)
    steps = (
        (up, xl, A, ur, 0, to_dn, ds, ur, 2),
        (dn, xl, B, dr, 0, to_up, us, dr, 2),
        (y, px, A, xr, 0, to_dn, ds, ur, 3),
        (up, xl, B, ur, 1, to_x, xs, xr, 2),
        (dn, xl, A, dr, 1, to_x, xs, xr, 3),
        (y, px, B, xr, 1, to_up, us, dr, 3),
        (op, xl, A, ur, 2, None, None, None, 0),
        (op, xl, B, dr, 2, None, None, None, 0),
        (up, px, A, ur, 3, to_dn, ds, ur, 4),
        (dn, px, B, dr, 3, to_up, us, dr, 4),
        (up, px, B, xr, 2, None, None, None, 0),
        (dn, px, A, xr, 3, None, None, None, 0),
        (op, px, A, ur, 4, None, None, None, 0),
        (op, px, B, dr, 4, None, None, None, 0),
    )
    for yy, xx, h, sems, i, target, ssems, rsems, j in steps:
        o = idx(yy, xx)
        arrived(o, h, sems.at[i])
        if target is not None:
            send(at(o, h), o, h, target, ssems.at[j], rsems.at[j])
        across(at(o, h), o, h)
    for i, (o, h) in enumerate(order):
        arrived(o + 1 - 2 * c, h, cr.at[i])
    for copy in sends:
        copy.wait_send()
    own.wait()


def gather_piece(x, members):
    sem = pltpu.SemaphoreType.DMA
    return pl.pallas_call(
        gather_kernel,
        out_shape=jax.ShapeDtypeStruct((members,) + x.shape, x.dtype),
        in_specs=[pl.BlockSpec(memory_space=pl.ANY)],
        out_specs=pl.BlockSpec(memory_space=pl.ANY),
        scratch_shapes=[
            sem, sem((5,)), sem((5,)), sem((4,)), sem((16,)),
            sem((5,)), sem((5,)), sem((4,)), sem((16,)), sem,
        ],
        compiler_params=pltpu.CompilerParams(collective_id=1, has_side_effects=True),
        name="gather_piece",
    )(x)


BLOCK = 512


def forward_kernel(kv_ref, q_ref, k_ref, v_ref, probs_ref, att_ref, scores, value_t):
    block = q_ref.shape[0]
    scale = HEAD_SIZE ** (-0.5)
    number = pl.program_id(1)

    @pl.when(jnp.logical_and(pl.program_id(0) == 0, number == 0))
    def _():
        value_t[...] = v_ref[...].astype(f32).T.astype(bf16)

    q = q_ref[...]
    above = lax.broadcasted_iota(jnp.int32, (block, block), 0) > lax.broadcasted_iota(
        jnp.int32, (block, block), 1
    )

    def rows(j):
        return pl.ds(pl.multiple_of(j * block, block), block)

    def score(j):
        return contraction(k_ref[rows(j), :], q, 1, 1) * scale

    def one(j, top):
        s = score(j)
        scores[rows(j), :] = s
        return jnp.maximum(top, jnp.max(s, axis=0, keepdims=True))

    s = jnp.where(above, neg_big, score(number))
    scores[rows(number), :] = s
    top = lax.fori_loop(0, number, one, jnp.max(s, axis=0, keepdims=True))

    def two(j, total):
        e = jnp.exp(scores[rows(j), :] - top)
        scores[rows(j), :] = e
        return total + jnp.sum(e, axis=0, keepdims=True)

    total = lax.fori_loop(0, number + 1, two, jnp.zeros((1, block), f32))
    share = 1.0 / total

    def three(j, acc):
        p = (scores[rows(j), :] * share).astype(bf16)
        probs_ref[0, 0, rows(j), :] = p
        return acc + jnp.dot(value_t[:, rows(j)], p, preferred_element_type=f32)

    acc = lax.fori_loop(0, number + 1, three, jnp.zeros((HEAD_SIZE, block), f32))
    att_ref[...] = acc.T.astype(bf16)


def attention_forward(kv_index, queries, keys, values):
    piece, cols = queries.shape
    heads = cols // HEAD_SIZE
    blocks = piece // BLOCK
    grid_spec = pltpu.PrefetchScalarGridSpec(
        num_scalar_prefetch=1,
        grid=(heads, blocks),
        in_specs=[
            pl.BlockSpec((BLOCK, HEAD_SIZE), lambda h, i, kv: (i, h)),
            pl.BlockSpec((piece, HEAD_SIZE), lambda h, i, kv: (0, kv[0])),
            pl.BlockSpec((piece, HEAD_SIZE), lambda h, i, kv: (0, kv[0])),
        ],
        out_specs=(
            pl.BlockSpec((1, 1, piece, BLOCK), lambda h, i, kv: (h, i, 0, 0)),
            pl.BlockSpec((BLOCK, HEAD_SIZE), lambda h, i, kv: (i, h)),
        ),
        scratch_shapes=[pltpu.VMEM((piece, BLOCK), f32), pltpu.VMEM((HEAD_SIZE, piece), bf16)],
    )
    return pl.pallas_call(
        forward_kernel,
        grid_spec=grid_spec,
        out_shape=(
            jax.ShapeDtypeStruct((heads, blocks, piece, BLOCK), bf16),
            jax.ShapeDtypeStruct((piece, cols), bf16),
        ),
        compiler_params=pltpu.CompilerParams(
            dimension_semantics=("arbitrary", "arbitrary"), vmem_limit_bytes=40 << 20
        ),
        cost_estimate=pl.CostEstimate(
            flops=20_000_000_000, bytes_accessed=40_000_000, transcendentals=5_000_000
        ),
        name="attention_forward",
    )(kv_index, queries, keys, values)


def backward_kernel(kv_ref, p_ref, q_ref, g_ref, att_ref, k_ref, v_ref, dq_ref, kv_out, key_t, key_sum, value_sum):
    block = q_ref.shape[0]
    scale = HEAD_SIZE ** (-0.5)
    head, number = pl.program_id(0), pl.program_id(1)

    @pl.when(jnp.logical_and(head == 0, number == 0))
    def _():
        key_t[...] = k_ref[...].astype(f32).T.astype(bf16)
        key_sum[...] = jnp.zeros_like(key_sum)
        value_sum[...] = jnp.zeros_like(value_sum)

    q = q_ref[...]
    g = g_ref[...]
    delta = jnp.sum((g.astype(f32) * att_ref[...].astype(f32)).T, axis=0, keepdims=True)

    def rows(j):
        return pl.ds(pl.multiple_of(j * block, block), block)

    def turn(j, acc):
        p = p_ref[0, 0, rows(j), :]
        grad = contraction(v_ref[rows(j), :], g, 1, 1)
        ds = (p.astype(f32) * (grad - delta)).astype(bf16)
        value_sum[rows(j), :] += jnp.dot(p, g, preferred_element_type=f32)
        key_sum[rows(j), :] += jnp.dot(ds, q, preferred_element_type=f32)
        return acc + jnp.dot(key_t[:, rows(j)], ds, preferred_element_type=f32)

    acc = lax.fori_loop(0, number + 1, turn, jnp.zeros((HEAD_SIZE, block), f32))
    dq_ref[...] = acc.T * scale

    @pl.when(jnp.logical_and(head == pl.num_programs(0) - 1, number == pl.num_programs(1) - 1))
    def _():
        kv_out[:, :HEAD_SIZE] = (key_sum[...] * scale).astype(bf16)
        kv_out[:, HEAD_SIZE:] = value_sum[...].astype(bf16)


def attention_backward(kv_index, probs, queries, grads, attended, keys, values):
    piece, cols = queries.shape
    heads = cols // HEAD_SIZE
    blocks = piece // BLOCK
    tile = pl.BlockSpec((BLOCK, HEAD_SIZE), lambda h, i, kv: (i, h))
    column = pl.BlockSpec((piece, HEAD_SIZE), lambda h, i, kv: (0, kv[0]))
    grid_spec = pltpu.PrefetchScalarGridSpec(
        num_scalar_prefetch=1,
        grid=(heads, blocks),
        in_specs=[
            pl.BlockSpec((1, 1, piece, BLOCK), lambda h, i, kv: (h, i, 0, 0)),
            tile,
            tile,
            tile,
            column,
            column,
        ],
        out_specs=(tile, pl.BlockSpec((piece, 2 * HEAD_SIZE), lambda h, i, kv: (0, 0))),
        scratch_shapes=[
            pltpu.VMEM((HEAD_SIZE, piece), bf16),
            pltpu.VMEM((piece, HEAD_SIZE), f32),
            pltpu.VMEM((piece, HEAD_SIZE), f32),
        ],
    )
    return pl.pallas_call(
        backward_kernel,
        grid_spec=grid_spec,
        out_shape=(
            jax.ShapeDtypeStruct((piece, cols), f32),
            jax.ShapeDtypeStruct((piece, 2 * HEAD_SIZE), bf16),
        ),
        compiler_params=pltpu.CompilerParams(
            dimension_semantics=("arbitrary", "arbitrary"), vmem_limit_bytes=40 << 20
        ),
        cost_estimate=pl.CostEstimate(
            flops=20_000_000_000, bytes_accessed=30_000_000, transcendentals=0
        ),
        name="attention_backward",
    )(kv_index, probs, queries, grads, attended, keys, values)


def exchange(x, axes):
    return lax.all_to_all(x, axes, split_axis=0, concat_axis=0, tiled=True)


def on_device(
    output_gradient,
    expert_choice_index,
    routing_weight,
    stored_gate_preact,
    gate_up_weight,
    down_weight,
    down_first_factor,
    down_second_factor,
    rotated_queries,
    rotated_keys,
    stored_values,
    output_weight,
    output_first_factor,
    output_second_factor,
):
    tok_rows, model_width = output_gradient.shape
    grp_count = lax.axis_size("grp")
    dev_count = lax.axis_size("dev")
    experts = grp_count * dev_count
    slot_count = stored_gate_preact.shape[1]
    capacity = slot_count // experts
    sub = model_width // 128
    piece_len, share_cols = rotated_queries.shape
    device_share = share_cols // HEAD_SIZE
    group_size = QUERY_HEADS // KVH
    rank_total = output_second_factor.shape[0]
    kv_index = (lax.axis_index("dev") * device_share // group_size).astype(jnp.int32).reshape(1)

    outgoing, cells = dispatch(
        output_gradient, expert_choice_index, routing_weight, experts, capacity
    )
    incoming = exchange(outgoing.reshape(experts, capacity, sub, 128), ALL)
    probs, attended = attention_forward(kv_index, rotated_queries, rotated_keys, stored_values)
    spread = jnp.zeros((device_share, rank_total, device_share, HEAD_SIZE), bf16)
    for h in range(device_share):
        spread = spread.at[h, :, h, :].set(
            output_first_factor[:, h * HEAD_SIZE : (h + 1) * HEAD_SIZE]
        )
    spread = spread.reshape(device_share * rank_total, share_cols)
    folded = contraction(attended, spread, 1, 1).astype(bf16)

    grad_rows, gradient_first, gradient_second = experts_backward(
        incoming.reshape(slot_count, sub, 128),
        stored_gate_preact[0],
        gate_up_weight[0],
        down_weight[0],
        down_first_factor[0],
        down_second_factor[0],
        256,
    )
    returned = exchange(grad_rows.reshape(experts, capacity, sub, 128), ALL)
    residual_gradient = combine(
        cells[:, : expert_choice_index.shape[1]],
        output_gradient,
        returned.reshape(slot_count, sub, 128),
    )
    segment_gradient = gather_piece(residual_gradient, dev_count).reshape(piece_len, model_width)

    lowrank_token = contraction(segment_gradient, output_second_factor, 1, 1).astype(bf16)
    head_gradient = (
        contraction(segment_gradient, output_weight, 1, 1)
        + adapter_scale * jnp.dot(lowrank_token, output_first_factor, preferred_element_type=f32)
    ).astype(bf16)
    row_contrib = (adapter_scale * contraction(lowrank_token, attended, 0, 0)).astype(bf16)
    column_contrib = contraction(folded, segment_gradient, 0, 0)
    column_contrib = adapter_scale * jnp.sum(
        column_contrib.reshape(device_share, rank_total, model_width), axis=0
    )

    tiles = column_contrib.reshape(rank_total // 8, 8, model_width // 128, 128)
    tiles = tiles.transpose(0, 2, 1, 3).reshape(experts, 8, 128)
    tile = jnp.sum(exchange(tiles, ALL), axis=0)
    tiles = exchange(jnp.broadcast_to(tile[None], (experts, 8, 128)), ALL)
    tiles = tiles.reshape(rank_total // 8, model_width // 128, 8, 128).transpose(0, 2, 1, 3)
    output_second_gradient = tiles.reshape(rank_total, model_width)
    row_all = exchange(jnp.broadcast_to(row_contrib[None], (grp_count,) + row_contrib.shape), "grp")
    output_first_gradient = jnp.sum(row_all.astype(f32), axis=0)

    query_gradient, kv_terms = attention_backward(
        kv_index, probs, rotated_queries, head_gradient, attended, rotated_keys, stored_values
    )
    kv_all = exchange(kv_terms.reshape(dev_count, tok_rows, 2 * HEAD_SIZE), "dev")
    kv_sum = jnp.sum(
        kv_all.reshape(KVH, dev_count // KVH, tok_rows, 2 * HEAD_SIZE).astype(f32), axis=1
    )
    key_gradient = kv_sum[:, :, :HEAD_SIZE].transpose(1, 0, 2).reshape(tok_rows, KVH * HEAD_SIZE)
    value_gradient = kv_sum[:, :, HEAD_SIZE:].transpose(1, 0, 2).reshape(tok_rows, KVH * HEAD_SIZE)
    return (
        gradient_first[None],
        gradient_second[None],
        residual_gradient,
        output_first_gradient,
        output_second_gradient,
        query_gradient,
        key_gradient,
        value_gradient,
    )


def solution(mesh):
    in_specs = (
        P(("grp", "dev"), None),
        P(("grp", "dev"), None),
        P(("grp", "dev"), None),
        P(("grp", "dev"), None, None),
        P(("grp", "dev"), None, None),
        P(("grp", "dev"), None, None),
        P(("grp", "dev"), None, None),
        P(("grp", "dev"), None, None),
        P("grp", "dev"),
        P("grp", None),
        P("grp", None),
        P("dev", None),
        P(None, "dev"),
        P(),
    )
    out_specs = (
        P(("grp", "dev"), None, None),
        P(("grp", "dev"), None, None),
        P(("grp", "dev"), None),
        P(None, "dev"),
        P(),
        P("grp", "dev"),
        P(("grp", "dev"), None),
        P(("grp", "dev"), None),
    )
    return jax.shard_map(
        on_device, mesh=mesh, in_specs=in_specs, out_specs=out_specs, check_vma=False
    )
```

time: 727 us -> 334 us (0.46)
  waiting for transfers between devices: 391 us -> 66.7 us
  Pallas kernels: 0 us -> 120 us
  matrix products: 108 us -> 17.8 us
  local copies, waits for them, and re-layouts: 84 us -> 15.9 us
  other arithmetic: 45.6 us -> 3.79 us
  blocking collectives: 38.8 us -> 75.9 us
  between operations: 14.9 us -> 0.88 us
    psum x1 -> x0, waiting for transfers between devices: 152 us -> none  [on_device(): lax.psum(adapter_scale * column_contrib, ('grp', 'dev'))]
    all_to_all x2 -> x5, waiting for transfers between devices: 196 us -> 66.7 us  [exchange(): return lax.all_to_all(x, axes, split_axis=0, concat_axis=0, tiled=True)]
    pallas_call x0 -> x6, Pallas kernels: none -> 120 us  [the longest x1 37.3 us: gather_piece(): pl.pallas_call(gather_kernel, out_shape=jax.ShapeDtypeStruct((members,) +...]
    all_to_all x0 -> x1, blocking collectives: none -> 75.9 us  [exchange(): return lax.all_to_all(x, axes, split_axis=0, concat_axis=0, tiled=True)]
    dot_general x30 -> x1, matrix products: 45.6 us -> 0.47 us  [on_device(): jnp.dot(lowrank_token, output_first_factor, preferred_element_type=f32)]
    reduce_scatter x2 -> x0, waiting for transfers between devices: 42.5 us -> none  [the longest x1 42.5 us: on_device(): lax.psum_scatter(value_term.astype(jnp.bfloat16), 'dev', scatter_dimensio...]
    psum x1 -> x0, blocking collectives: 38.8 us -> none  [on_device(): lax.psum((adapter_scale * row_contrib).astype(jnp.bfloat16), 'grp')]
    reshape x4 -> x0, local copies, waits for them, and re-layouts: 38.7 us -> none  [the longest x1 9.83 us: on_device(): routed_rows = incoming.reshape(slot_count, model_width)]
  transfers between devices with their start and end apart: 6 -> 5, of which waited for: 4 -> 3; matrix products, arithmetic and copies ran while one was open for 15% -> 5% of each run, Pallas kernels for 0% -> 11%
where the time goes in v1:
time: 334 us; the launch traced here: 333 us
  Pallas kernels  120 us (36%)
  blocking collectives  75.9 us (23%)
  waiting for transfers between devices  66.7 us (20%)
  starting transfers between devices  31.6 us (9%)
  matrix products  17.8 us (5%)
  local copies, waits for them, and re-layouts  15.9 us (5%)
  other arithmetic  3.79 us (1%)
    all_to_all x1, blocking collectives, exchange(): return lax.all_to_all(x, axes, split_axis=0, concat_axis=0, tiled=True)  75.9 us
    all_to_all x5, waiting for transfers between devices, exchange(): return lax.all_to_all(x, axes, split_axis=0, concat_axis=0, tiled=True)  66.7 us
    pallas_call x1, Pallas kernels, gather_piece(): pl.pallas_call(gather_kernel, out_shape=jax.ShapeDtypeStruct((members,) +...  37.3 us
    all_to_all x5, starting transfers between devices, exchange(): return lax.all_to_all(x, axes, split_axis=0, concat_axis=0, tiled=True)  31.6 us
    pallas_call x1, Pallas kernels, experts_backward(): pl.pallas_call(expert_kernel, grid=(slots // count,), out_shape=(jax.Shap...  31 us
    pallas_call x1, Pallas kernels, attention_backward(): pl.pallas_call(backward_kernel, grid_spec=grid_spec, out_shape=(jax.Shape...  19.8 us
    pallas_call x1, Pallas kernels, attention_forward(): pl.pallas_call(forward_kernel, grid_spec=grid_spec, out_shape=(jax.ShapeD...  18.2 us
    dot_general x5, matrix products, contraction(): lax.dot_general(left, right, (((left_dim,), (right_dim,)), ((), ())), pre...  17.4 us
  transfers between devices with their start and end apart: 5, of which 3 were waited for; matrix products, arithmetic and copies ran while one was open for 5% of the time, Pallas kernels for 11%

profile of v1, /device:TPU:1, one launch (start us, length us, event | category | flops | bytes accessed | tf_op | source)
XLA Modules:
  0.0 332.7 jit_solution(1021372475270007781)
XLA Ops:
  0.6 0.0 copy-start
  0.6 1.5 copy.37.idx_ref
  2.2 1.4 copy.38.w_ref
  3.6 8.6 %dispatch.1 = (bf16[1280,16,128]{2,1,0:T(8,128)(2,1)}, s32[128,128]{1,0:T(8,128)}) custom-call(bf16[128,2048]{1,0:T(8,128)(2,1)} %x_ref.3, s32[128,8]{1,0:T(8,128)} %copy.37.idx_ref, f32[128,8]{1,0:T(8,128)} %copy.38.w_ref), custom_call_target="tpu_custom_call" | custom-call | tf_op jit(solution)/shard_map/dispatch/pallas_call | solution.py:88
  12.2 75.9 %all_to_all.30 = bf16[128,10,16,128]{3,2,1,0:T(8,128)(2,1)} all-to-all(bf16[128,10,16,128]{3,2,1,0:T(8,128)(2,1)} %bitcast.62), channel_id=1, replica_groups=mesh['grp'=8,'dev'=16] {'grp','dev'}, dimensions={0} | all-to-all | bytes 10485760 | tf_op jit(solution)/shard_map/all_to_all | solution.py:491
  88.1 31.0 %experts.1 = (bf16[1280,16,128]{2,1,0:T(8,128)(2,1)}, f32[64,768]{1,0:T(8,128)}, f32[64,2048]{1,0:T(8,128)}) custom-call(bf16[1280,16,128]{2,1,0:T(8,128)(2,1)} %bitcast.63, bf16[1280,1536]{1,0:T(8,128)(2,1)} %bitcast.72, bf16[2048,1536]{1,0:T(8,128)(2,1)} %bitcast.71, bf16[768,2048]{1,0:T(8,128)(2,1)} %bitcast.73, bf16[64,768]{1,0:T(8,128)(2,1)} %bitcast.75, ...), custom_call_target="tpu_custom_call" | custom-call | flops 13500000256 | bytes 24000000 | tf_op jit(solution)/shard_map/experts/pallas_call | solution.py:159
  119.2 5.5 %all-to-all-start.1 = ((bf16[128,10,16,128]{3,2,1,0:T(8,128)(2,1)}), bf16[128,10,16,128]{3,2,1,0:T(8,128)(2,1)}, u32[]{:S(2)}, u32[]{:S(2)}) async-start(bf16[128,10,16,128]{3,2,1,0:T(8,128)(2,1)} %bitcast.61), calls=%async_computation.1 | async-start | bytes 10485760 | tf_op jit(solution)/shard_map/all_to_all | solution.py:491
  124.7 0.0 copy-done.9
  124.8 0.1 copy.39
  124.9 0.0 copy-done.6
  124.9 0.0 copy-start.2
  124.9 1.6 copy-done.2
  126.5 1.6 copy-done.4
  128.1 18.2 %attention_forward.1 = (bf16[2,4,2048,512]{3,2,1,0:T(8,128)(2,1)}, bf16[2048,256]{1,0:T(8,128)(2,1)S(1)}) custom-call(s32[1]{0:T(128)} %bitcast.12.kv_ref, bf16[2048,256]{1,0:T(8,128)(2,1)S(1)} %copy-done.6, bf16[2048,512]{1,0:T(8,128)(2,1)S(1)} %copy-done.2, bf16[2048,512]{1,0:T(8,128)(2,1)S(1)} %copy-done.4), custom_call_target="tpu_custom_call" | custom-call | flops 20000000000 | bytes 40000000 | tf_op jit(solution)/shard_map/attention_forward/pallas_call | solution.py:397
  146.2 0.5 convolution_convert_fusion
  146.7 42.0 %all-to-all-done.1 = bf16[128,10,16,128]{3,2,1,0:T(8,128)(2,1)} async-done(((bf16[128,10,16,128]{3,2,1,0:T(8,128)(2,1)}), bf16[128,10,16,128]{3,2,1,0:T(8,128)(2,1)}, u32[]{:S(2)}, u32[]{:S(2)}) %all-to-all-start.1) | async-done | bytes 5242912 | tf_op jit(solution)/shard_map/all_to_all | solution.py:491
  188.7 5.2 %combine.1.x_ref = bf16[128,2048]{1,0:T(8,128)(2,1)} custom-call(s32[128,8]{1,0:T(8,128)} %bitcast.70, bf16[128,2048]{1,0:T(8,128)(2,1)} %x_ref.3, bf16[1280,16,128]{2,1,0:T(8,128)(2,1)} %bitcast.10.r_ref), custom_call_target="tpu_custom_call" | custom-call | tf_op jit(solution)/shard_map/combine/pallas_call | solution.py:211
  193.9 37.3 %gather_piece.1 = bf16[16,128,2048]{2,1,0:T(8,128)(2,1)} custom-call(bf16[128,2048]{1,0:T(8,128)(2,1)} %combine.1.x_ref), custom_call_target="tpu_custom_call" | custom-call | tf_op jit(solution)/shard_map/gather_piece/pallas_call | solution.py:316
  231.3 6.0 %convolution_convert_fusion.1 = bf16[2048,64]{0,1:T(8,128)(2,1)S(1)} fusion(bf16[2048,2048]{1,0:T(8,128)(2,1)} %bitcast.58, bf16[64,2048]{1,0:T(8,128)(2,1)S(1)} %copy-done.8), kind=kOutput, calls=%fused_computation.4 | convolution fusion | flops 537001984 | bytes 8912896 | tf_op jit(solution)/shard_map/dot_general | solution.py:23
  237.3 0.3 fusion.2
  237.6 0.7 broadcast_in_dim.10
  238.3 4.2 %all-to-all-start.2 = ((bf16[8,64,256]{2,1,0:T(8,128)(2,1)}), bf16[8,64,256]{2,1,0:T(8,128)(2,1)}, u32[]{:S(2)}, u32[]{:S(2)}) async-start(bf16[8,64,256]{2,1,0:T(8,128)(2,1)} %broadcast_in_dim.10), calls=%async_computation.2 | async-start | bytes 524288 | tf_op jit(solution)/shard_map/all_to_all | solution.py:491
  242.6 4.7 %convolution_reduce_fusion = f32[64,2048]{1,0:T(8,128)S(1)} fusion(bf16[2,64,2048]{2,1,0:T(8,128)(2,1)S(1)} %bitcast.64, bf16[2048,2048,1]{1,0,2:T(8,128)(2,1)} %bitcast.59), kind=kOutput, calls=%fused_computation.6 | convolution fusion | flops 1073872896 | bytes 9437184 | tf_op jit(solution)/shard_map/dot_general | solution.py:23
  247.2 0.8 broadcast_multiply_fusion
  248.1 5.9 %fusion.5 = f32[2048,256]{1,0:T(8,128)S(1)} fusion(bf16[2048,2048]{1,0:T(8,128)(2,1)} %bitcast.60, bf16[256,2048]{1,0:T(8,128)(2,1)S(1)} %copy-done), kind=kOutput, calls=%fused_computation.17 | convolution fusion | flops 2147483648 | bytes 11534336 | tf_op jit(solution)/shard_map/dot_general | solution.py:23
  254.0 0.5 fusion.1.g_ref
  254.4 0.0 all-to-all-done.2
  254.5 8.3 %all-to-all-start.3 = ((f32[128,8,128]{2,1,0:T(8,128)}), f32[128,8,128]{2,1,0:T(8,128)}, u32[]{:S(2)}, u32[]{:S(2)}) async-start(f32[128,8,128]{2,1,0:T(8,128)} %bitcast.66), calls=%async_computation.3 | async-start | bytes 1048576 | tf_op jit(solution)/shard_map/all_to_all | solution.py:491
  262.8 0.0 copy-start.3
  262.8 1.6 copy-done.3
  264.4 1.6 copy-done.5
  266.0 1.2 copy-done.7
  267.2 19.8 %attention_backward.1 = (f32[2048,256]{1,0:T(8,128)}, bf16[2048,256]{1,0:T(8,128)(2,1)S(1)}) custom-call(s32[1]{0:T(128)} %bitcast.12.kv_ref, bf16[2,4,2048,512]{3,2,1,0:T(8,128)(2,1)} %get-tuple-element.47.p_ref, bf16[2048,256]{1,0:T(8,128)(2,1)S(1)} %copy-done.7, bf16[2048,256]{1,0:T(8,128)(2,1)S(1)} %fusion.1.g_ref, ...), custom_call_target="tpu_custom_call" | custom-call | flops 20000000000 | bytes 30000000 | tf_op jit(solution)/shard_map/attention_backward/pallas_call | solution.py:473
  287.0 1.0 copy-done.1
  288.0 0.0 all-to-all-done.3
  288.0 5.7 %all-to-all-start.5 = ((bf16[16,128,256]{2,1,0:T(8,128)(2,1)}), bf16[16,128,256]{2,1,0:T(8,128)(2,1)S(1)}, u32[]{:S(2)}, u32[]{:S(2)}) async-start(bf16[16,128,256]{2,1,0:T(8,128)(2,1)} %bitcast.57), calls=%async_computation.5 | async-start | bytes 2097152 | tf_op jit(solution)/shard_map/all_to_all | solution.py:491
  293.7 1.2 reduce_sum.38
  294.9 14.5 %all-to-all-done.5 = bf16[16,128,256]{2,1,0:T(8,128)(2,1)S(1)} async-done(((bf16[16,128,256]{2,1,0:T(8,128)(2,1)}), bf16[16,128,256]{2,1,0:T(8,128)(2,1)S(1)}, u32[]{:S(2)}, u32[]{:S(2)}) %all-to-all-start.5) | async-done | bytes 1048608 | tf_op jit(solution)/shard_map/all_to_all | solution.py:491
  309.4 0.8 broadcast_in_dim.22
  310.2 7.8 %all-to-all-start.4 = ((f32[128,8,128]{2,1,0:T(8,128)}), f32[128,8,128]{2,1,0:T(8,128)S(1)}, u32[]{:S(2)}, u32[]{:S(2)}) async-start(f32[128,8,128]{2,1,0:T(8,128)} %broadcast_in_dim.22), calls=%async_computation.4 | async-start | bytes 1048576 | tf_op jit(solution)/shard_map/all_to_all | solution.py:491
  318.0 1.6 convert_reduce_fusion.1
  319.6 0.2 convert_reduce_fusion
  319.8 0.1 copy.40
  320.0 0.8 copy.42
  320.8 0.1 copy.41
  320.9 0.8 copy.43
  321.8 10.2 %all-to-all-done.4 = f32[128,8,128]{2,1,0:T(8,128)S(1)} async-done(((f32[128,8,128]{2,1,0:T(8,128)}), f32[128,8,128]{2,1,0:T(8,128)S(1)}, u32[]{:S(2)}, u32[]{:S(2)}) %all-to-all-start.4) | async-done | bytes 524320 | tf_op jit(solution)/shard_map/all_to_all | solution.py:491
  331.9 0.8 copy.51
  (13 shorter events, 0.1 us)
Async XLA Ops:
  0.6 247.4 %copy-start = (bf16[256,2048]{1,0:T(8,128)(2,1)S(1)}, bf16[256,2048]{1,0:T(8,128)(2,1)}, u32[]{:S(2)}) copy-start(bf16[256,2048]{1,0:T(8,128)(2,1)} %param.29) | copy-start | bytes 3145732
  119.2 5.6 %copy-start.9 = (bf16[64,256]{1,0:T(8,128)(2,1)S(1)}, bf16[64,256]{1,0:T(8,128)(2,1)}, u32[]{:S(2)}) copy-start(bf16[64,256]{1,0:T(8,128)(2,1)} %param.30) | copy-start | bytes 98308
  119.2 5.7 %copy-start.6 = (bf16[2048,256]{1,0:T(8,128)(2,1)S(1)}, bf16[2048,256]{1,0:T(8,128)(2,1)}, u32[]{:S(2)}) copy-start(bf16[2048,256]{1,0:T(8,128)(2,1)} %q_ref.3) | copy-start | bytes 3145732
  119.2 69.6 %all-to-all-start.1 = ((bf16[128,10,16,128]{3,2,1,0:T(8,128)(2,1)}), bf16[128,10,16,128]{3,2,1,0:T(8,128)(2,1)}, u32[]{:S(2)}, u32[]{:S(2)}) async-start(bf16[128,10,16,128]{3,2,1,0:T(8,128)(2,1)} %bitcast.61), calls=%async_computation.1 | async-start | bytes 10485760 | tf_op jit(solution)/shard_map/all_to_all | solution.py:491
  124.9 1.6 copy-start.2
  126.5 1.6 copy-start.4
  193.9 37.3 %copy-start.8 = (bf16[64,2048]{1,0:T(8,128)(2,1)S(1)}, bf16[64,2048]{1,0:T(8,128)(2,1)}, u32[]{:S(2)}) copy-start(bf16[64,2048]{1,0:T(8,128)(2,1)} %param.31) | copy-start | bytes 786436
  238.3 16.1 %all-to-all-start.2 = ((bf16[8,64,256]{2,1,0:T(8,128)(2,1)}), bf16[8,64,256]{2,1,0:T(8,128)(2,1)}, u32[]{:S(2)}, u32[]{:S(2)}) async-start(bf16[8,64,256]{2,1,0:T(8,128)(2,1)} %broadcast_in_dim.10), calls=%async_computation.2 | async-start | bytes 524288 | tf_op jit(solution)/shard_map/all_to_all | solution.py:491
  254.5 33.5 %all-to-all-start.3 = ((f32[128,8,128]{2,1,0:T(8,128)}), f32[128,8,128]{2,1,0:T(8,128)}, u32[]{:S(2)}, u32[]{:S(2)}) async-start(f32[128,8,128]{2,1,0:T(8,128)} %bitcast.66), calls=%async_computation.3 | async-start | bytes 1048576 | tf_op jit(solution)/shard_map/all_to_all | solution.py:491
  262.8 1.6 copy-start.3
  264.4 1.6 copy-start.5
  266.0 1.2 copy-start.7
  287.0 1.0 copy-start.1
  288.0 21.4 %all-to-all-start.5 = ((bf16[16,128,256]{2,1,0:T(8,128)(2,1)}), bf16[16,128,256]{2,1,0:T(8,128)(2,1)S(1)}, u32[]{:S(2)}, u32[]{:S(2)}) async-start(bf16[16,128,256]{2,1,0:T(8,128)(2,1)} %bitcast.57), calls=%async_computation.5 | async-start | bytes 2097152 | tf_op jit(solution)/shard_map/all_to_all | solution.py:491
  310.2 21.7 %all-to-all-start.4 = ((f32[128,8,128]{2,1,0:T(8,128)}), f32[128,8,128]{2,1,0:T(8,128)S(1)}, u32[]{:S(2)}, u32[]{:S(2)}) async-start(f32[128,8,128]{2,1,0:T(8,128)} %broadcast_in_dim.22), calls=%async_computation.4 | async-start | bytes 1048576 | tf_op jit(solution)/shard_map/all_to_all | solution.py:491

commit v2 on v1

v2 whole, which is shorter than its diff:
```python
import functools

import jax
import jax.numpy as jnp
from jax import lax
from jax.experimental import pallas as pl
from jax.experimental.pallas import tpu as pltpu
from jax.sharding import PartitionSpec as P

QUERY_HEADS = 32
KVH = 4
HEAD_SIZE = 128
MESH = pl.DeviceIdType.MESH
ALL = ("grp", "dev")

adapter_scale = 2.0
neg_big = -1e30
f32 = jnp.float32
bf16 = jnp.bfloat16


def contraction(left, right, left_dim, right_dim):
    return lax.dot_general(
        left, right, (((left_dim,), (right_dim,)), ((), ())), preferred_element_type=f32
    )


def dispatch_kernel(capacity, x_ref, idx_ref, w_ref, out_ref, cells_ref, rows, tok_v, wt_v, tok_s, wt_s, sems):
    tokens, width = x_ref.shape
    sub = width // 128
    per_step = out_ref.shape[0] // capacity
    step = pl.program_id(0)

    @pl.when(step == 0)
    def _():
        for b in range(sub):
            rows[pl.ds(b, tokens, stride=sub), :] = x_ref[:, b * 128 : (b + 1) * 128].astype(f32)
        shape = tok_v.shape
        e_iota = lax.broadcasted_iota(jnp.int32, shape, 0)
        t_iota = lax.broadcasted_iota(jnp.int32, shape, 1)
        idx = idx_ref[...]
        w = w_ref[...]
        named = jnp.zeros(shape, f32)
        weight = jnp.zeros(shape, f32)
        for k in range(idx.shape[0]):
            hit = idx[k : k + 1, :] == e_iota
            named = named + jnp.where(hit, 1.0, 0.0)
            weight = weight + jnp.where(hit, w[k : k + 1, :], 0.0)
        earlier = jnp.where(e_iota < t_iota, 1.0, 0.0).astype(bf16)
        rank = jnp.dot(named.astype(bf16), earlier, preferred_element_type=f32)
        t_float = t_iota.astype(f32)
        toks = jnp.zeros(shape, f32)
        wts = jnp.zeros(shape, f32)
        for c in range(capacity):
            mine = jnp.logical_and(named > 0.5, rank == float(c))
            tok = jnp.sum(jnp.where(mine, t_float, 0.0), axis=1, keepdims=True)
            wt = jnp.sum(jnp.where(mine, weight, 0.0), axis=1, keepdims=True)
            toks = jnp.where(t_iota == c, tok, toks)
            wts = jnp.where(t_iota == c, wt, wts)
        tok_v[...] = toks.astype(jnp.int32)
        wt_v[...] = wts
        for k in range(idx.shape[0]):
            hit = idx[k : k + 1, :] == e_iota
            place = jnp.sum(jnp.where(hit, rank, 0.0), axis=0, keepdims=True)
            cells_ref[k : k + 1, :] = place.astype(jnp.int32) + capacity * idx[k : k + 1, :]
        one = pltpu.make_async_copy(tok_v, tok_s, sems.at[0])
        two = pltpu.make_async_copy(wt_v, wt_s, sems.at[1])
        one.start()
        two.start()
        one.wait()
        two.wait()

    def expert(j, carry):
        e = step * per_step + j
        for c in range(capacity):
            start = pl.multiple_of(tok_s[e, c] * sub, sub)
            out_ref[j * capacity + c] = (rows[pl.ds(start, sub), :] * wt_s[e, c]).astype(bf16)
        return carry

    lax.fori_loop(0, per_step, expert, 0, unroll=2)


def dispatch(x, idx, w, experts, capacity):
    tokens, width = x.shape
    sub = width // 128
    steps = 8
    slots = experts * capacity
    idx, w = idx.T, w.T
    return pl.pallas_call(
        functools.partial(dispatch_kernel, capacity),
        grid=(steps,),
        out_shape=(
            jax.ShapeDtypeStruct((slots, sub, 128), bf16),
            jax.ShapeDtypeStruct(idx.shape, jnp.int32),
        ),
        in_specs=[
            pl.BlockSpec((tokens, width), lambda i: (0, 0)),
            pl.BlockSpec(idx.shape, lambda i: (0, 0)),
            pl.BlockSpec(w.shape, lambda i: (0, 0)),
        ],
        out_specs=(
            pl.BlockSpec((slots // steps, sub, 128), lambda i: (i, 0, 0)),
            pl.BlockSpec(idx.shape, lambda i: (0, 0)),
        ),
        scratch_shapes=[
            pltpu.VMEM((tokens * sub, 128), f32),
            pltpu.VMEM((experts, tokens), jnp.int32),
            pltpu.VMEM((experts, tokens), f32),
            pltpu.SMEM((experts, tokens), jnp.int32),
            pltpu.SMEM((experts, tokens), f32),
            pltpu.SemaphoreType.DMA((2,)),
        ],
        compiler_params=pltpu.CompilerParams(dimension_semantics=("arbitrary",)),
        name="dispatch",
    )(x, idx, w)


def expert_kernel(r_ref, s_ref, g_ref, d_ref, a_ref, b_ref, out_ref, first_ref, second_ref, wide, rows):
    count, sub, _ = r_ref.shape
    ff = d_ref.shape[0]

    @pl.when(pl.program_id(0) == 0)
    def _():
        first_ref[...] = jnp.zeros_like(first_ref)
        second_ref[...] = jnp.zeros_like(second_ref)

    wide[...] = r_ref[...].astype(f32).reshape(count * sub, 128)
    for b in range(sub):
        rows[:, b * 128 : (b + 1) * 128] = wide[pl.ds(b, count, stride=sub), :].astype(bf16)
    x = rows[...]
    pre_gate = s_ref[:, :ff].astype(f32)
    pre_up = s_ref[:, ff:].astype(f32)
    sigmoid = jax.nn.sigmoid(pre_gate)
    activated = pre_gate * sigmoid
    slope = sigmoid * (1.0 + pre_gate * (1.0 - sigmoid))
    hidden = (activated * pre_up).astype(bf16)
    low_in = contraction(hidden, a_ref[...], 1, 1).astype(bf16)
    low_grad = contraction(x, b_ref[...], 1, 1).astype(bf16)
    second_ref[...] += adapter_scale * contraction(low_in, x, 0, 0)
    first_ref[...] += adapter_scale * contraction(low_grad, hidden, 0, 0)
    grad_hidden = contraction(x, d_ref[...], 1, 1) + adapter_scale * jnp.dot(
        low_grad, a_ref[...], preferred_element_type=f32
    )
    left = (grad_hidden * (pre_up * slope)).astype(bf16)
    right = (grad_hidden * activated).astype(bf16)
    for b in range(0, sub, 2):
        at = slice(b * 128, (b + 2) * 128)
        res = contraction(left, g_ref[at, :ff], 1, 1) + contraction(right, g_ref[at, ff:], 1, 1)
        wide[pl.ds(b, count, stride=sub), :] = res[:, :128]
        wide[pl.ds(b + 1, count, stride=sub), :] = res[:, 128:]
    out_ref[...] = wide[...].reshape(count, sub, 128).astype(bf16)


def experts_backward(routed, saved, gate_up, down, first, second, count):
    slots, sub, _ = routed.shape
    ff, width = down.shape
    rank = first.shape[0]
    once = pl.Buffered(1)
    whole = lambda shape: pl.BlockSpec(shape, lambda i: (0, 0), pipeline_mode=once)
    return pl.pallas_call(
        expert_kernel,
        grid=(slots // count,),
        out_shape=(
            jax.ShapeDtypeStruct((slots, sub, 128), bf16),
            jax.ShapeDtypeStruct((rank, ff), f32),
            jax.ShapeDtypeStruct((rank, width), f32),
        ),
        in_specs=[
            pl.BlockSpec((count, sub, 128), lambda i: (i, 0, 0)),
            pl.BlockSpec((count, 2 * ff), lambda i: (i, 0)),
            whole(gate_up.shape),
            whole(down.shape),
            whole(first.shape),
            whole(second.shape),
        ],
        out_specs=(
            pl.BlockSpec((count, sub, 128), lambda i: (i, 0, 0)),
            pl.BlockSpec((rank, ff), lambda i: (0, 0)),
            pl.BlockSpec((rank, width), lambda i: (0, 0)),
        ),
        scratch_shapes=[pltpu.VMEM((count * sub, 128), f32), pltpu.VMEM((count, width), bf16)],
        compiler_params=pltpu.CompilerParams(
            dimension_semantics=("arbitrary",), vmem_limit_bytes=56 << 20
        ),
        cost_estimate=pl.CostEstimate(flops=13_500_000_000, bytes_accessed=24_000_000, transcendentals=0),
        name="experts",
    )(routed, saved, gate_up, down, first, second)


def combine_kernel(cells_ref, x_ref, r_ref, s_ref, out_ref, col_ref, rows):
    tokens, width = x_ref.shape
    sub = width // 128
    top = cells_ref.shape[0]

    def token(t, carry):
        total = r_ref[cells_ref[0, t]].astype(f32)
        for k in range(1, top):
            total = total + r_ref[cells_ref[k, t]].astype(f32)
        rows[pl.ds(pl.multiple_of(t * sub, sub), sub), :] = total
        return carry

    lax.fori_loop(0, tokens, token, 0, unroll=4)
    share = s_ref[...]
    high = share.astype(bf16)
    low = (share - high.astype(f32)).astype(bf16)
    for b in range(sub):
        at = slice(b * 128, (b + 1) * 128)
        res = (x_ref[:, at].astype(f32) + rows[pl.ds(b, tokens, stride=sub), :]).astype(bf16)
        out_ref[:, at] = res
        col_ref[:, at] = adapter_scale * (
            jnp.dot(high, res, preferred_element_type=f32)
            + jnp.dot(low, res, preferred_element_type=f32)
        )


def combine(cells, x, returned, share):
    tokens, width = x.shape
    vmem = pl.BlockSpec(memory_space=pltpu.VMEM)
    return pl.pallas_call(
        combine_kernel,
        out_shape=(
            jax.ShapeDtypeStruct(x.shape, bf16),
            jax.ShapeDtypeStruct((share.shape[0], width), f32),
        ),
        in_specs=[pl.BlockSpec(memory_space=pltpu.SMEM), vmem, vmem, vmem],
        out_specs=(vmem, vmem),
        scratch_shapes=[pltpu.VMEM((tokens * width // 128, 128), f32)],
        name="combine",
    )(cells, x, returned, share)


def remote(src, dst, ssem, rsem, target):
    return pltpu.make_async_remote_copy(
        src_ref=src, dst_ref=dst, send_sem=ssem, recv_sem=rsem,
        device_id=target, device_id_type=MESH,
    )


def greet(targets):
    barrier = pltpu.get_barrier_semaphore()
    for target in targets:
        pl.semaphore_signal(barrier, inc=1, device_id=target, device_id_type=MESH)
    pl.semaphore_wait(barrier, len(targets))


def share_kernel(devs, s_ref, out_ref, box, ssem, rsem, lsem):
    g = lax.axis_index("grp")
    d = lax.axis_index("dev")
    peers = [(g, (d + i) % devs) for i in range(1, devs)]
    greet(peers)

    def block(i):
        return s_ref.at[:, pl.ds(pl.multiple_of(i * 128, 128), 128)]

    for peer in peers:
        remote(block(peer[1]), box.at[d], ssem, rsem, peer).start()
    own = pltpu.make_async_copy(block(d), box.at[d], lsem)
    own.start()
    own.wait()
    part = box.at[pl.ds(0, devs - 1)]
    both = remote(part, part, ssem, rsem, peers[0])
    both.wait_send()
    both.wait_recv()
    total = box[0]
    for i in range(1, devs):
        total = total + box[i]
    out_ref[...] = total


def share_tokens(folded, devs):
    rank, piece = folded.shape
    sem = pltpu.SemaphoreType.DMA
    vmem = pl.BlockSpec(memory_space=pltpu.VMEM)
    return pl.pallas_call(
        functools.partial(share_kernel, devs),
        out_shape=jax.ShapeDtypeStruct((rank, piece // devs), f32),
        in_specs=[vmem],
        out_specs=vmem,
        scratch_shapes=[pltpu.VMEM((devs, rank, piece // devs), f32), sem, sem, sem],
        compiler_params=pltpu.CompilerParams(collective_id=2, has_side_effects=True),
        name="share_tokens",
    )(folded)


def gather_kernel(
    grps, devs, x_ref, col_ref, y_ref, tot_ref,
    spare, us, ds, xs, cs, ur, dr, xr, cr, lsem,
    box1, part, box2, tile, full, s1, r1, s2, r2, s3, r3, s4, r4, l4,
):
    g = lax.axis_index("grp")
    d = lax.axis_index("dev")
    y = d // 4
    xl = (d // 2) % 2
    c = d % 2
    half = x_ref.shape[0] // 2

    def idx(yy, xx):
        return yy * 4 + xx * 2 + c

    px = 1 - xl
    up, dn, op = (y + 1) % 4, (y + 3) % 4, (y + 2) % 4
    to_up, to_dn, to_x = (g, idx(up, xl)), (g, idx(dn, xl)), (g, idx(y, px))
    to_c = (g, y * 4 + xl * 2 + (1 - c))
    dev_peers = [(g, (d + i) % devs) for i in range(1, devs)]
    grp_peers = [((g + i) % grps, d) for i in range(1, grps)]
    greet(dev_peers + grp_peers)
    A, B = 0, 1
    rows = col_ref.shape[0] // grps

    def part_of(h):
        return x_ref.at[pl.ds(h * half, half)]

    def at(o, h):
        return y_ref.at[o, pl.ds(h * half, half)]

    def band(ref, i):
        return ref.at[pl.ds(pl.multiple_of(i * rows, rows), rows)]

    def lanes(ref, i):
        return ref.at[:, pl.ds(pl.multiple_of(i * 128, 128), 128)]

    mine = idx(y, xl)
    sends = []
    order = []

    def send(src, o, h, target, ssem, rsem):
        copy = remote(src, at(o, h), ssem, rsem, target)
        copy.start()
        sends.append(copy)

    def arrived(o, h, sem):
        remote(at(o, h), at(o, h), spare, sem, to_c).wait_recv()

    def across(src, o, h):
        i = len(order)
        order.append((o, h))
        send(src, o, h, to_c, cs.at[i], cr.at[i])

    own = pltpu.make_async_copy(x_ref, y_ref.at[mine], lsem)
    own.start()
    send(part_of(A), mine, A, to_dn, ds.at[0], ur.at[0])
    send(part_of(B), mine, B, to_up, us.at[0], dr.at[0])
    send(part_of(A), mine, A, to_x, xs.at[0], xr.at[0])
    send(part_of(B), mine, B, to_dn, ds.at[1], ur.at[1])
    send(part_of(A), mine, A, to_up, us.at[1], dr.at[1])
    send(part_of(B), mine, B, to_x, xs.at[1], xr.at[1])
    across(part_of(A), mine, A)
    across(part_of(B), mine, B)
    for peer in grp_peers:
        remote(band(col_ref, peer[0]), box1.at[g], s1, r1, peer).start()

    def settle(ref, count, ssem, rsem):
        whole = remote(ref.at[pl.ds(0, count)], ref.at[pl.ds(0, count)], ssem, rsem, to_c)
        whole.wait_send()
        whole.wait_recv()

    def round_two():
        settle(box1, grps - 1, s1, r1)
        box1[g] = band(col_ref, g)[...]
        total = box1[0]
        for i in range(1, grps):
            total = total + box1[i]
        part[...] = total
        for peer in dev_peers:
            remote(lanes(part, peer[1]), box2.at[d], s2, r2, peer).start()

    def round_three():
        settle(box2, devs - 1, s2, r2)
        box2[d] = lanes(part, d)[...]
        total = box2[0]
        for i in range(1, devs):
            total = total + box2[i]
        tile[...] = total
        for peer in dev_peers:
            remote(tile, full.at[d], s3, r3, peer).start()

    def round_four():
        settle(full, devs - 1, s3, r3)
        full[d] = tile[...]
        for i in range(devs):
            part[:, i * 128 : (i + 1) * 128] = full[i]
        for peer in grp_peers:
            remote(part, band(tot_ref, g), s4, r4, peer).start()
        last = pltpu.make_async_copy(part, band(tot_ref, g), l4)
        last.start()
        last.wait()

    steps = (
        (up, xl, A, ur, 0, to_dn, ds, ur, 2),
        (dn, xl, B, dr, 0, to_up, us, dr, 2),
        (y, px, A, xr, 0, to_dn, ds, ur, 3),
        (up, xl, B, ur, 1, to_x, xs, xr, 2),
        (dn, xl, A, dr, 1, to_x, xs, xr, 3),
        (y, px, B, xr, 1, to_up, us, dr, 3),
        (op, xl, A, ur, 2, None, None, None, 0),
        (op, xl, B, dr, 2, None, None, None, 0),
        (up, px, A, ur, 3, to_dn, ds, ur, 4),
        (dn, px, B, dr, 3, to_up, us, dr, 4),
        round_two,
        (up, px, B, xr, 2, None, None, None, 0),
        (dn, px, A, xr, 3, None, None, None, 0),
        round_three,
        (op, px, A, ur, 4, None, None, None, 0),
        (op, px, B, dr, 4, None, None, None, 0),
        round_four,
    )
    for step in steps:
        if callable(step):
            step()
            continue
        yy, xx, h, sems, i, target, ssems, rsems, j = step
        o = idx(yy, xx)
        arrived(o, h, sems.at[i])
        if target is not None:
            send(at(o, h), o, h, target, ssems.at[j], rsems.at[j])
        across(at(o, h), o, h)
    for i, (o, h) in enumerate(order):
        arrived(o + 1 - 2 * c, h, cr.at[i])
    for copy in sends:
        copy.wait_send()
    own.wait()
    others = tot_ref.at[pl.ds(0, rows * (grps - 1))]
    rest = remote(others, others, s4, r4, to_c)
    rest.wait_send()
    rest.wait_recv()


def gather_piece(x, col, grps, devs):
    sem = pltpu.SemaphoreType.DMA
    rows = col.shape[0] // grps
    vmem = pl.BlockSpec(memory_space=pltpu.VMEM)
    hbm = pl.BlockSpec(memory_space=pl.ANY)
    return pl.pallas_call(
        functools.partial(gather_kernel, grps, devs),
        out_shape=(
            jax.ShapeDtypeStruct((devs,) + x.shape, x.dtype),
            jax.ShapeDtypeStruct(col.shape, f32),
        ),
        in_specs=[hbm, vmem],
        out_specs=(hbm, vmem),
        scratch_shapes=[
            sem, sem((5,)), sem((5,)), sem((4,)), sem((16,)),
            sem((5,)), sem((5,)), sem((4,)), sem((16,)), sem,
            pltpu.VMEM((grps, rows, col.shape[1]), f32),
            pltpu.VMEM((rows, col.shape[1]), f32),
            pltpu.VMEM((devs, rows, 128), f32),
            pltpu.VMEM((rows, 128), f32),
            pltpu.VMEM((devs, rows, 128), f32),
            sem, sem, sem, sem, sem, sem, sem, sem, sem,
        ],
        compiler_params=pltpu.CompilerParams(collective_id=1, has_side_effects=True),
        name="gather_piece",
    )(x, col)


def finish_kernel(
    grps, devs, kv_ref, row_ref, box, rbox,
    other, total, cs, cr, ssem, rsem, s2, r2, lsem,
):
    g = lax.axis_index("grp")
    d = lax.axis_index("dev")
    y = d // 4
    c = d % 2
    chip = d // 2
    chips = devs // 2
    partner = (g, d + 1 - 2 * c)
    dev_peers = [(g, (d + i) % devs) for i in range(1, devs)]
    grp_peers = [((g + i) % grps, d) for i in range(1, grps)]
    greet(dev_peers + grp_peers)
    block = box.shape[1]
    span = 4 * block

    def rows(i, size):
        return pl.ds(pl.multiple_of(i * size, size), size)

    chunks = [(y + 2) % 4, (y + 1) % 4, (y + 3) % 4, y]
    swaps = []
    for i, j in enumerate(chunks):
        copy = remote(
            kv_ref.at[1 - c, rows(j, span)], other.at[rows(j, span)], cs.at[i], cr.at[i], partner
        )
        copy.start()
        swaps.append(copy)
    for peer in grp_peers:
        remote(row_ref, rbox.at[g], s2, r2, peer).start()
    for i, j in enumerate(chunks):
        swaps[i].wait_recv()
        at = rows(j, span)
        total[at, :] = (kv_ref[c, at, :].astype(f32) + other[at, :].astype(f32)).astype(bf16)
        for k in range(4):
            e = j * 4 + k
            src = total.at[rows(e, block)]
            if i < 3:
                remote(src, box.at[c * chips + chip], ssem, rsem, (g, e)).start()
            else:

                @pl.when(e != d)
                def _():
                    remote(src, box.at[c * chips + chip], ssem, rsem, (g, e)).start()

    mine = pltpu.make_async_copy(total.at[rows(d, block)], box.at[c * chips + chip], lsem)
    mine.start()
    mine.wait()
    for copy in swaps:
        copy.wait_send()
    some = rbox.at[pl.ds(0, grps - 1)]
    both = remote(some, some, s2, r2, partner)
    both.wait_send()
    both.wait_recv()
    rbox[g] = row_ref[...]
    some = box.at[pl.ds(0, devs - 1)]
    both = remote(some, some, ssem, rsem, partner)
    both.wait_send()
    both.wait_recv()


def totals_kernel(box, rbox, all_ref, key_ref, value_ref, first_ref, second_ref):
    chips = box.shape[0] // 2
    per = chips // KVH
    acc = rbox[0].astype(f32)
    for i in range(1, rbox.shape[0]):
        acc = acc + rbox[i].astype(f32)
    first_ref[...] = acc
    for kind, out in ((0, key_ref), (1, value_ref)):
        for m in range(KVH):
            acc = box[kind * chips + m * per].astype(f32)
            for i in range(1, per):
                acc = acc + box[kind * chips + m * per + i].astype(f32)
            out[:, m * HEAD_SIZE : (m + 1) * HEAD_SIZE] = acc
    second_ref[...] = all_ref[...]


def finish(kv, row, columns, grps, devs):
    piece = kv.shape[1]
    block = piece // devs
    sem = pltpu.SemaphoreType.DMA
    vmem = pl.BlockSpec(memory_space=pltpu.VMEM)
    box, rbox = pl.pallas_call(
        functools.partial(finish_kernel, grps, devs),
        out_shape=(
            jax.ShapeDtypeStruct((devs, block, HEAD_SIZE), bf16),
            jax.ShapeDtypeStruct((grps,) + row.shape, bf16),
        ),
        in_specs=[vmem, vmem],
        out_specs=(vmem, vmem),
        scratch_shapes=[
            pltpu.VMEM((piece, HEAD_SIZE), bf16),
            pltpu.VMEM((piece, HEAD_SIZE), bf16),
            sem((4,)), sem((4,)), sem, sem, sem, sem, sem,
        ],
        compiler_params=pltpu.CompilerParams(collective_id=3, has_side_effects=True),
        name="finish",
    )(kv, row)
    side = jax.ShapeDtypeStruct((block, KVH * HEAD_SIZE), f32)
    return pl.pallas_call(
        totals_kernel,
        out_shape=(
            side,
            side,
            jax.ShapeDtypeStruct(row.shape, f32),
            jax.ShapeDtypeStruct(columns.shape, f32),
        ),
        in_specs=[vmem, vmem, vmem],
        out_specs=(vmem, vmem, vmem, vmem),
        name="totals",
    )(box, rbox, columns)


BLOCK = 512


def forward_kernel(kv_ref, q_ref, k_ref, v_ref, f_ref, probs_ref, att_ref, fold_ref, scores, value_t):
    block = q_ref.shape[0]
    scale = HEAD_SIZE ** (-0.5)
    number = pl.program_id(1)

    @pl.when(jnp.logical_and(pl.program_id(0) == 0, number == 0))
    def _():
        value_t[...] = v_ref[...].astype(f32).T.astype(bf16)

    q = q_ref[...]
    above = lax.broadcasted_iota(jnp.int32, (block, block), 0) > lax.broadcasted_iota(
        jnp.int32, (block, block), 1
    )

    def rows(j):
        return pl.ds(pl.multiple_of(j * block, block), block)

    def score(j):
        return contraction(k_ref[rows(j), :], q, 1, 1) * scale

    def one(j, top):
        s = score(j)
        scores[rows(j), :] = s
        return jnp.maximum(top, jnp.max(s, axis=0, keepdims=True))

    s = jnp.where(above, neg_big, score(number))
    scores[rows(number), :] = s
    top = lax.fori_loop(0, number, one, jnp.max(s, axis=0, keepdims=True))

    def two(j, total):
        e = jnp.exp(scores[rows(j), :] - top)
        scores[rows(j), :] = e
        return total + jnp.sum(e, axis=0, keepdims=True)

    total = lax.fori_loop(0, number + 1, two, jnp.zeros((1, block), f32))
    share = 1.0 / total

    def three(j, acc):
        p = (scores[rows(j), :] * share).astype(bf16)
        probs_ref[0, 0, rows(j), :] = p
        return acc + jnp.dot(value_t[:, rows(j)], p, preferred_element_type=f32)

    acc = lax.fori_loop(0, number + 1, three, jnp.zeros((HEAD_SIZE, block), f32))
    att_ref[...] = acc.T.astype(bf16)
    fold = jnp.dot(f_ref[...], acc.astype(bf16), preferred_element_type=f32)
    fold = fold.astype(bf16).astype(f32)
    at = rows(number)

    @pl.when(pl.program_id(0) == 0)
    def _():
        fold_ref[:, at] = fold

    @pl.when(pl.program_id(0) > 0)
    def _():
        fold_ref[:, at] += fold


def attention_forward(kv_index, queries, keys, values, factor):
    piece, cols = queries.shape
    heads = cols // HEAD_SIZE
    blocks = piece // BLOCK
    grid_spec = pltpu.PrefetchScalarGridSpec(
        num_scalar_prefetch=1,
        grid=(heads, blocks),
        in_specs=[
            pl.BlockSpec((BLOCK, HEAD_SIZE), lambda h, i, kv: (i, h)),
            pl.BlockSpec((piece, HEAD_SIZE), lambda h, i, kv: (0, kv[0])),
            pl.BlockSpec((piece, HEAD_SIZE), lambda h, i, kv: (0, kv[0])),
            pl.BlockSpec((factor.shape[0], HEAD_SIZE), lambda h, i, kv: (0, h)),
        ],
        out_specs=(
            pl.BlockSpec((1, 1, piece, BLOCK), lambda h, i, kv: (h, i, 0, 0)),
            pl.BlockSpec((BLOCK, HEAD_SIZE), lambda h, i, kv: (i, h)),
            pl.BlockSpec((factor.shape[0], piece), lambda h, i, kv: (0, 0)),
        ),
        scratch_shapes=[pltpu.VMEM((piece, BLOCK), f32), pltpu.VMEM((HEAD_SIZE, piece), bf16)],
    )
    return pl.pallas_call(
        forward_kernel,
        grid_spec=grid_spec,
        out_shape=(
            jax.ShapeDtypeStruct((heads, blocks, piece, BLOCK), bf16),
            jax.ShapeDtypeStruct((piece, cols), bf16),
            jax.ShapeDtypeStruct((factor.shape[0], piece), f32),
        ),
        compiler_params=pltpu.CompilerParams(
            dimension_semantics=("arbitrary", "arbitrary"), vmem_limit_bytes=40 << 20
        ),
        cost_estimate=pl.CostEstimate(
            flops=20_000_000_000, bytes_accessed=40_000_000, transcendentals=5_000_000
        ),
        name="attention_forward",
    )(kv_index, queries, keys, values, factor)


def backward_kernel(
    kv_ref, p_ref, q_ref, seg_ref, att_ref, k_ref, v_ref, w_ref, f1_ref, f2_ref,
    dq_ref, kv_out, row_ref, key_t, key_sum, value_sum, grads, row_sum,
):
    block = q_ref.shape[0]
    scale = HEAD_SIZE ** (-0.5)
    number, head = pl.program_id(0), pl.program_id(1)
    heads = grads.shape[0]

    @pl.when(jnp.logical_and(head == 0, number == 0))
    def _():
        key_t[...] = k_ref[...].astype(f32).T.astype(bf16)
        key_sum[...] = jnp.zeros_like(key_sum)
        value_sum[...] = jnp.zeros_like(value_sum)
        row_sum[...] = jnp.zeros_like(row_sum)

    @pl.when(head == 0)
    def _():
        seg = seg_ref[...]
        low = contraction(seg, f2_ref[...], 1, 1).astype(bf16)
        full = contraction(seg, w_ref[...], 1, 1) + adapter_scale * jnp.dot(
            low, f1_ref[...], preferred_element_type=f32
        )
        for h in range(heads):
            grads[h] = full[:, h * HEAD_SIZE : (h + 1) * HEAD_SIZE].astype(bf16)
        row_sum[...] += contraction(low, att_ref[...], 0, 0)

    q = q_ref[...]
    g = grads[head]
    att = att_ref[:, pl.ds(pl.multiple_of(head * HEAD_SIZE, HEAD_SIZE), HEAD_SIZE)]
    delta = jnp.sum((g.astype(f32) * att.astype(f32)).T, axis=0, keepdims=True)

    def rows(j):
        return pl.ds(pl.multiple_of(j * block, block), block)

    def turn(j, acc):
        p = p_ref[0, 0, rows(j), :]
        grad = contraction(v_ref[rows(j), :], g, 1, 1)
        ds = (p.astype(f32) * (grad - delta)).astype(bf16)
        value_sum[rows(j), :] += jnp.dot(p, g, preferred_element_type=f32)
        key_sum[rows(j), :] += jnp.dot(ds, q, preferred_element_type=f32)
        return acc + jnp.dot(key_t[:, rows(j)], ds, preferred_element_type=f32)

    acc = lax.fori_loop(0, number + 1, turn, jnp.zeros((HEAD_SIZE, block), f32))
    dq_ref[...] = acc.T * scale

    @pl.when(jnp.logical_and(head == pl.num_programs(1) - 1, number == pl.num_programs(0) - 1))
    def _():
        kv_out[0] = (key_sum[...] * scale).astype(bf16)
        kv_out[1] = value_sum[...].astype(bf16)
        row_ref[...] = (adapter_scale * row_sum[...]).astype(bf16)


def attention_backward(kv_index, probs, queries, segment, attended, keys, values, weight, first, second):
    piece, cols = queries.shape
    heads = cols // HEAD_SIZE
    blocks = piece // BLOCK
    once = pl.Buffered(1)
    tile = pl.BlockSpec((BLOCK, HEAD_SIZE), lambda i, h, kv: (i, h))
    column = pl.BlockSpec((piece, HEAD_SIZE), lambda i, h, kv: (0, kv[0]), pipeline_mode=once)
    whole = lambda a: pl.BlockSpec(a.shape, lambda i, h, kv: (0, 0), pipeline_mode=once)
    grid_spec = pltpu.PrefetchScalarGridSpec(
        num_scalar_prefetch=1,
        grid=(blocks, heads),
        in_specs=[
            pl.BlockSpec((1, 1, piece, BLOCK), lambda i, h, kv: (h, i, 0, 0)),
            tile,
            pl.BlockSpec((BLOCK, segment.shape[1]), lambda i, h, kv: (i, 0)),
            pl.BlockSpec((BLOCK, cols), lambda i, h, kv: (i, 0)),
            column,
            column,
            whole(weight),
            whole(first),
            whole(second),
        ],
        out_specs=(
            tile,
            pl.BlockSpec((2, piece, HEAD_SIZE), lambda i, h, kv: (0, 0, 0)),
            pl.BlockSpec(first.shape, lambda i, h, kv: (0, 0)),
        ),
        scratch_shapes=[
            pltpu.VMEM((HEAD_SIZE, piece), bf16),
            pltpu.VMEM((piece, HEAD_SIZE), f32),
            pltpu.VMEM((piece, HEAD_SIZE), f32),
            pltpu.VMEM((heads, BLOCK, HEAD_SIZE), bf16),
            pltpu.VMEM(first.shape, f32),
        ],
    )
    return pl.pallas_call(
        backward_kernel,
        grid_spec=grid_spec,
        out_shape=(
            jax.ShapeDtypeStruct((piece, cols), f32),
            jax.ShapeDtypeStruct((2, piece, HEAD_SIZE), bf16),
            jax.ShapeDtypeStruct(first.shape, bf16),
        ),
        compiler_params=pltpu.CompilerParams(
            dimension_semantics=("arbitrary", "arbitrary"), vmem_limit_bytes=48 << 20
        ),
        cost_estimate=pl.CostEstimate(
            flops=20_000_000_000, bytes_accessed=40_000_000, transcendentals=0
        ),
        name="attention_backward",
    )(kv_index, probs, queries, segment, attended, keys, values, weight, first, second)


def exchange(x, axes):
    return lax.all_to_all(x, axes, split_axis=0, concat_axis=0, tiled=True)


def on_device(
    output_gradient,
    expert_choice_index,
    routing_weight,
    stored_gate_preact,
    gate_up_weight,
    down_weight,
    down_first_factor,
    down_second_factor,
    rotated_queries,
    rotated_keys,
    stored_values,
    output_weight,
    output_first_factor,
    output_second_factor,
):
    tok_rows, model_width = output_gradient.shape
    grp_count = lax.axis_size("grp")
    dev_count = lax.axis_size("dev")
    experts = grp_count * dev_count
    slot_count = stored_gate_preact.shape[1]
    capacity = slot_count // experts
    sub = model_width // 128
    piece_len, share_cols = rotated_queries.shape
    device_share = share_cols // HEAD_SIZE
    group_size = QUERY_HEADS // KVH
    kv_index = (lax.axis_index("dev") * device_share // group_size).astype(jnp.int32).reshape(1)

    outgoing, cells = dispatch(
        output_gradient, expert_choice_index, routing_weight, experts, capacity
    )
    incoming = exchange(outgoing.reshape(experts, capacity, sub, 128), ALL)
    probs, attended, folded = attention_forward(
        kv_index, rotated_queries, rotated_keys, stored_values, output_first_factor
    )
    share = share_tokens(folded, dev_count)

    grad_rows, gradient_first, gradient_second = experts_backward(
        incoming.reshape(slot_count, sub, 128),
        stored_gate_preact[0],
        gate_up_weight[0],
        down_weight[0],
        down_first_factor[0],
        down_second_factor[0],
        256,
    )
    returned = exchange(grad_rows.reshape(experts, capacity, sub, 128), ALL)
    residual_gradient, column_contrib = combine(
        cells,
        output_gradient,
        returned.reshape(slot_count, sub, 128),
        share,
    )
    segment_gradient, columns = gather_piece(
        residual_gradient, column_contrib, grp_count, dev_count
    )
    query_gradient, kv_terms, row_contrib = attention_backward(
        kv_index,
        probs,
        rotated_queries,
        segment_gradient.reshape(piece_len, model_width),
        attended,
        rotated_keys,
        stored_values,
        output_weight,
        output_first_factor,
        output_second_factor,
    )
    key_gradient, value_gradient, output_first_gradient, output_second_gradient = finish(
        kv_terms, row_contrib, columns, grp_count, dev_count
    )
    return (
        gradient_first[None],
        gradient_second[None],
        residual_gradient,
        output_first_gradient,
        output_second_gradient,
        query_gradient,
        key_gradient,
        value_gradient,
    )


def solution(mesh):
    in_specs = (
        P(("grp", "dev"), None),
        P(("grp", "dev"), None),
        P(("grp", "dev"), None),
        P(("grp", "dev"), None, None),
        P(("grp", "dev"), None, None),
        P(("grp", "dev"), None, None),
        P(("grp", "dev"), None, None),
        P(("grp", "dev"), None, None),
        P("grp", "dev"),
        P("grp", None),
        P("grp", None),
        P("dev", None),
        P(None, "dev"),
        P(),
    )
    out_specs = (
        P(("grp", "dev"), None, None),
        P(("grp", "dev"), None, None),
        P(("grp", "dev"), None),
        P(None, "dev"),
        P(),
        P("grp", "dev"),
        P(("grp", "dev"), None),
        P(("grp", "dev"), None),
    )
    return jax.shard_map(
        on_device, mesh=mesh, in_specs=in_specs, out_specs=out_specs, check_vma=False
    )
```

time: 334 us -> 302 us (0.904)
  Pallas kernels: 120 us -> 213 us
  waiting for transfers between devices: 66.7 us -> 0.01 us
  starting transfers between devices: 31.6 us -> 5.71 us
  matrix products: 17.8 us -> 0 us
  local copies, waits for them, and re-layouts: 15.9 us -> 6.19 us
  other arithmetic: 3.79 us -> 0 us
    pallas_call x2 -> x5, Pallas kernels: 42.5 us -> 122 us  [the longest x1 53.5 us: gather_piece(): pl.pallas_call(functools.partial(gather_kernel, grps, devs), out_shape=(j...]
    all_to_all x5 -> x1, waiting for transfers between devices: 66.7 us -> 0.01 us  [exchange(): return lax.all_to_all(x, axes, split_axis=0, concat_axis=0, tiled=True)]
    all_to_all x5 -> x1, starting transfers between devices: 31.6 us -> 5.71 us  [exchange(): return lax.all_to_all(x, axes, split_axis=0, concat_axis=0, tiled=True)]
    dot_general x6 -> x0, matrix products: 17.8 us -> none  [the longest x5 17.4 us: contraction(): lax.dot_general(left, right, (((left_dim,), (right_dim,)), ((), ())), pre...]
    pallas_call x1, Pallas kernels: 19.8 us -> 31.5 us  [attention_backward(): pl.pallas_call(backward_kernel, grid_spec=grid_spec, out_shape=(jax.Shape...]
    unnamed x25 -> x22, local copies, waits for them, and re-layouts: 14 us -> 6.19 us
  transfers between devices with their start and end apart: 5 -> 1, of which waited for: 3 -> 0; matrix products, arithmetic and copies ran while one was open for 5% -> 0% of each run, Pallas kernels for 11% -> 21%
where the time goes in v2:
time: 302 us
  Pallas kernels  213 us (71%)
  blocking collectives  75.9 us (25%)
  local copies, waits for them, and re-layouts  6.19 us (2%)
  starting transfers between devices  5.71 us (2%)
    all_to_all x1, blocking collectives, exchange(): return lax.all_to_all(x, axes, split_axis=0, concat_axis=0, tiled=True)  75.9 us
    pallas_call x1, Pallas kernels, gather_piece(): pl.pallas_call(functools.partial(gather_kernel, grps, devs), out_shape=(j...  53.5 us
    pallas_call x1, Pallas kernels, share_tokens(): pl.pallas_call(functools.partial(share_kernel, devs), out_shape=jax.Shape...  43.7 us
    pallas_call x1, Pallas kernels, attention_backward(): pl.pallas_call(backward_kernel, grid_spec=grid_spec, out_shape=(jax.Shape...  31.5 us
    pallas_call x1, Pallas kernels, experts_backward(): pl.pallas_call(expert_kernel, grid=(slots // count,), out_shape=(jax.Shap...  31.1 us
    pallas_call x1, Pallas kernels, attention_forward(): pl.pallas_call(forward_kernel, grid_spec=grid_spec, out_shape=(jax.ShapeD...  18.9 us
    pallas_call x1, Pallas kernels, finish(): pl.pallas_call(functools.partial(finish_kernel, grps, devs), out_shape=(j...  16.6 us
    pallas_call x1, Pallas kernels, dispatch(): pl.pallas_call(functools.partial(dispatch_kernel, capacity), grid=(steps,...  9.79 us
  transfers between devices with their start and end apart: 1, of which 0 were waited for; matrix products, arithmetic and copies ran while one was open for 0% of the time, Pallas kernels for 21%

profile of v2, /device:TPU:1, one launch (start us, length us, event | category | flops | bytes accessed | tf_op | source)
XLA Modules:
  0.0 301.6 jit_solution(15045321118973066874)
XLA Ops:
  0.6 9.8 %dispatch.1 = (bf16[1280,16,128]{2,1,0:T(8,128)(2,1)}, s32[8,128]{1,0:T(8,128)}) custom-call(bf16[128,2048]{1,0:T(8,128)(2,1)} %x_ref.3, s32[8,128]{1,0:T(8,128)} %bitcast.18, f32[8,128]{1,0:T(8,128)} %bitcast.19), custom_call_target="tpu_custom_call" | custom-call | tf_op jit(solution)/shard_map/dispatch/pallas_call | solution.py:89
  10.4 75.9 %all_to_all.10 = bf16[128,10,16,128]{3,2,1,0:T(8,128)(2,1)} all-to-all(bf16[128,10,16,128]{3,2,1,0:T(8,128)(2,1)} %bitcast.17), channel_id=1, replica_groups=mesh['grp'=8,'dev'=16] {'grp','dev'}, dimensions={0} | all-to-all | bytes 10485760 | tf_op jit(solution)/shard_map/all_to_all | solution.py:774
  86.3 31.1 %experts.1 = (bf16[1280,16,128]{2,1,0:T(8,128)(2,1)}, f32[64,768]{1,0:T(8,128)}, f32[64,2048]{1,0:T(8,128)}) custom-call(bf16[1280,16,128]{2,1,0:T(8,128)(2,1)} %bitcast.16, bf16[1280,1536]{1,0:T(8,128)(2,1)} %bitcast.22, bf16[2048,1536]{1,0:T(8,128)(2,1)} %bitcast.21, bf16[768,2048]{1,0:T(8,128)(2,1)} %bitcast.23, bf16[64,768]{1,0:T(8,128)(2,1)} %bitcast.25, ...), custom_call_target="tpu_custom_call" | custom-call | flops 13500000256 | bytes 24000000 | tf_op jit(solution)/shard_map/experts/pallas_call | solution.py:160
  117.4 0.0 copy-start.3
  117.4 0.0 copy-start.5
  117.4 0.0 copy-start.8
  117.4 5.7 %all-to-all-start.1 = ((bf16[128,10,16,128]{3,2,1,0:T(8,128)(2,1)}), bf16[128,10,16,128]{3,2,1,0:T(8,128)(2,1)}, u32[]{:S(2)}, u32[]{:S(2)}) async-start(bf16[128,10,16,128]{3,2,1,0:T(8,128)(2,1)} %bitcast.15), calls=%async_computation.1 | async-start | bytes 10485760 | tf_op jit(solution)/shard_map/all_to_all | solution.py:774
  123.1 0.0 copy-done.3
  123.2 0.0 copy-done.5
  123.2 0.0 copy-done.8
  123.2 0.0 copy-start.4
  123.2 1.6 copy-done.4
  124.8 18.9 %attention_forward.1 = (bf16[2,4,2048,512]{3,2,1,0:T(8,128)(2,1)}, bf16[2048,256]{1,0:T(8,128)(2,1)S(1)}, f32[64,2048]{1,0:T(8,128)S(1)}) custom-call(s32[1]{0:T(128)} %bitcast.13.kv_ref, bf16[2048,256]{1,0:T(8,128)(2,1)S(1)} %copy-done.5, bf16[2048,512]{1,0:T(8,128)(2,1)S(1)} %copy-done.3, bf16[2048,512]{1,0:T(8,128)(2,1)S(1)} %copy-done.4, ...), custom_call_target="tpu_custom_call" | custom-call | flops 20000000000 | bytes 40000000 | tf_op jit(solution)/shard_map/attention_forward/pallas_call | solution.py:649
  143.7 0.0 copy-start.1
  143.7 0.8 copy-done.1
  144.5 0.0 copy-start.9
  144.5 1.0 copy-done.9
  145.5 0.0 copy-start.6
  145.5 0.0 copy-start.7
  145.5 43.7 %share_tokens.1.s_ref = f32[64,128]{1,0:T(8,128)} custom-call(f32[64,2048]{1,0:T(8,128)} %copy-done.1), custom_call_target="tpu_custom_call" | custom-call | tf_op jit(solution)/shard_map/share_tokens/pallas_call | solution.py:274
  189.2 0.0 all-to-all-done.1
  189.2 5.6 %combine.1 = (bf16[128,2048]{1,0:T(8,128)(2,1)}, f32[64,2048]{1,0:T(8,128)}) custom-call(s32[8,128]{1,0:T(8,128)} %get-tuple-element.32.cells_ref, bf16[128,2048]{1,0:T(8,128)(2,1)} %x_ref.3, bf16[1280,16,128]{2,1,0:T(8,128)(2,1)} %bitcast.12.r_ref, f32[64,128]{1,0:T(8,128)} %share_tokens.1.s_ref), custom_call_target="tpu_custom_call" | custom-call | tf_op jit(solution)/shard_map/combine/pallas_call | solution.py:219
  194.8 53.5 %gather_piece.1 = (bf16[16,128,2048]{2,1,0:T(8,128)(2,1)}, f32[64,2048]{1,0:T(8,128)}) custom-call(bf16[128,2048]{1,0:T(8,128)(2,1)} %get-tuple-element.23.x_ref, f32[64,2048]{1,0:T(8,128)} %get-tuple-element.37.col_ref), custom_call_target="tpu_custom_call" | custom-call | tf_op jit(solution)/shard_map/gather_piece/pallas_call | solution.py:433
  248.3 0.0 copy-done.6
  248.3 0.0 copy-done.7
  248.3 0.0 copy-start.10
  248.3 1.2 copy-done.10
  249.6 31.5 %attention_backward.1 = (f32[2048,256]{1,0:T(8,128)}, bf16[2,2048,128]{2,1,0:T(8,128)(2,1)S(1)}, bf16[64,256]{1,0:T(8,128)(2,1)S(1)}) custom-call(s32[1]{0:T(128)} %bitcast.13.kv_ref, bf16[2,4,2048,512]{3,2,1,0:T(8,128)(2,1)} %get-tuple-element.36.p_ref, bf16[2048,256]{1,0:T(8,128)(2,1)S(1)} %copy-done.5, bf16[2048,2048]{1,0:T(8,128)(2,1)} %bitcast.20, ...), custom_call_target="tpu_custom_call" | custom-call | flops 20000000000 | bytes 40000000 | tf_op jit(solution)/shard_map/attention_backward/pallas_call | solution.py:755
  281.1 0.0 copy-start
  281.1 1.0 copy-done
  282.1 0.0 copy-start.2
  282.1 0.6 copy-done.2
  282.7 16.6 %finish.1 = (bf16[16,128,128]{2,1,0:T(8,128)(2,1)}, bf16[8,64,256]{2,1,0:T(8,128)(2,1)}) custom-call(bf16[2,2048,128]{2,1,0:T(8,128)(2,1)} %copy-done, bf16[64,256]{1,0:T(8,128)(2,1)} %copy-done.2), custom_call_target="tpu_custom_call" | custom-call | tf_op jit(solution)/shard_map/finish/pallas_call | solution.py:538
  299.3 2.3 totals.1
Async XLA Ops:
  117.4 5.8 %copy-start.3 = (bf16[2048,512]{1,0:T(8,128)(2,1)S(1)}, bf16[2048,512]{1,0:T(8,128)(2,1)}, u32[]{:S(2)}) copy-start(bf16[2048,512]{1,0:T(8,128)(2,1)} %k_ref.3) | copy-start | bytes 6291460
  117.4 5.8 %copy-start.5 = (bf16[2048,256]{1,0:T(8,128)(2,1)S(1)}, bf16[2048,256]{1,0:T(8,128)(2,1)}, u32[]{:S(2)}) copy-start(bf16[2048,256]{1,0:T(8,128)(2,1)} %q_ref.3) | copy-start | bytes 3145732
  117.4 5.8 %copy-start.8 = (bf16[64,256]{1,0:T(8,128)(2,1)S(1)}, bf16[64,256]{1,0:T(8,128)(2,1)}, u32[]{:S(2)}) copy-start(bf16[64,256]{1,0:T(8,128)(2,1)} %f1_ref.1) | copy-start | bytes 98308
  117.4 71.8 %all-to-all-start.1 = ((bf16[128,10,16,128]{3,2,1,0:T(8,128)(2,1)}), bf16[128,10,16,128]{3,2,1,0:T(8,128)(2,1)}, u32[]{:S(2)}, u32[]{:S(2)}) async-start(bf16[128,10,16,128]{3,2,1,0:T(8,128)(2,1)} %bitcast.15), calls=%async_computation.1 | async-start | bytes 10485760 | tf_op jit(solution)/shard_map/all_to_all | solution.py:774
  123.2 1.6 copy-start.4
  143.7 0.8 copy-start.1
  144.5 1.0 copy-start.9
  145.5 102.8 %copy-start.6 = (bf16[256,2048]{1,0:T(8,128)(2,1)S(1)}, bf16[256,2048]{1,0:T(8,128)(2,1)}, u32[]{:S(2)}) copy-start(bf16[256,2048]{1,0:T(8,128)(2,1)} %w_ref.1) | copy-start | bytes 3145732
  145.5 102.9 %copy-start.7 = (bf16[64,2048]{1,0:T(8,128)(2,1)S(1)}, bf16[64,2048]{1,0:T(8,128)(2,1)}, u32[]{:S(2)}) copy-start(bf16[64,2048]{1,0:T(8,128)(2,1)} %f2_ref.1) | copy-start | bytes 786436
  248.3 1.2 copy-start.10
  281.1 1.0 copy-start
  282.1 0.6 copy-start.2
